TPU v7x, 128 devices: a whole 4x4x4 slice. The times are simulated.
128 devices in a mesh: pipe: 8 (over y, x_lo), dp: 16 (over x_hi, z, core).
Axes of the slice: x: 4 (x_hi: 2, x_lo: 2; x = x_hi * 2 + x_lo), y: 4, z: 4, core: 2. Of those that a mesh axis runs over, the one named last changes fastest.
Arguments:
- clips: bfloat16 [2, 3, 2048, 1536], P(None, None, 'dp'), may hold values from -6 to 6
- positions: int32 [3, 2, 3, 2048], P(None, None, None, 'dp'), may hold values from 0 to 79, as said below
- out_proj: bfloat16 [8, 1536, 1536], P('pipe', 'dp'), may hold values from -0.15625 to 0.15625
- qk_gains: bfloat16 [8, 2, 128], P('pipe'), may hold values from -1.5 to 1.5
- cotangent: bfloat16 [2, 3, 2048, 1536], P(None, None, 'dp'), may hold values from -0.125 to 0.125
Outputs:
- grad_out_proj: float32 [8, 1536, 1536], P('pipe', 'dp')
- grad_gains: float32 [8, 2, 128], P('pipe')
Inputs may be any that keep to these rules, and one draw needn't show every extreme that they name: positions[0] is a token's frame, positions[1] its row and positions[2] its column in the latent video.
All inputs are finite; a program needn't handle non-finite values.
Results may differ from a plain program's by a relative error of at most 0.018.
Values may be sent and summed in bfloat16 or wider, within the bound.
A program may use at most 192 MiB of HBM per device.

v0:
```python
import math

import jax
import jax.numpy as jnp
from jax import lax
from jax.sharding import PartitionSpec as P


def from_partner(x, axis, distance):
    return lax.ppermute(x, axis, [(i, i ^ 1 << distance) for i in range(lax.axis_size(axis))])


def shifted(block, axis, distance):
    devices = range(lax.axis_size(axis))
    route = [(i - distance, i) for i in devices if i - distance in devices]
    return lax.ppermute(block, axis, route)


def rotate(values, coords):
    head_size = values.shape[-1]
    first_width = head_size // 8
    rest_width = (head_size - first_width) // 2
    widths = (first_width, rest_width, rest_width)
    pieces = []
    offset = 0
    for axis_index in range(3):
        section = widths[axis_index]
        half_width = section // 2
        segment = values[..., offset : offset + section]
        frequency = 256.0 ** (-2.0 * jnp.arange(half_width, dtype=jnp.float32) / section)
        angles = coords[axis_index].astype(jnp.float32)[:, None] * frequency[None, :]
        cosine = jnp.cos(angles)[:, None, :]
        sine_part = jnp.sin(angles)[:, None, :]
        lower_half = segment[..., :half_width]
        upper_half = segment[..., half_width:]
        pieces.append(lower_half * cosine - upper_half * sine_part)
        pieces.append(lower_half * sine_part + upper_half * cosine)
        offset = offset + section
    return jnp.concatenate(pieces, axis=-1)


def mixing(hidden, gain_pair, coords):
    row_count, channels = hidden.shape
    head_size = gain_pair.shape[-1]
    by_heads = hidden.reshape(row_count, channels // head_size, head_size)
    wide_heads = by_heads.astype(jnp.float32)
    normed = wide_heads * lax.rsqrt(
        jnp.mean(wide_heads * wide_heads, axis=-1, keepdims=True) + 1e-06
    )
    queries = rotate(normed * gain_pair[0], coords)
    key_rows = rotate(normed * gain_pair[1], coords)
    scores = jnp.einsum(
        "qhe,khe->hqk", queries, key_rows, precision=lax.Precision.HIGHEST
    ) / math.sqrt(head_size)
    exp_scores = jnp.exp(scores)
    weights = (exp_scores / jnp.sum(exp_scores, axis=-1, keepdims=True)).astype(jnp.bfloat16)
    weights_wide = lax.optimization_barrier(weights).astype(jnp.float32)
    mixed_rows = jnp.einsum("hqk,khe->qhe", weights_wide, wide_heads)
    return mixed_rows.reshape(row_count, channels).astype(jnp.bfloat16)


def phase_forward(hidden, gain_pair, coords, weight):
    mixed_rows = mixing(hidden, gain_pair, coords)
    update = jnp.dot(mixed_rows, weight, preferred_element_type=jnp.float32)
    return (hidden.astype(jnp.float32) + update).astype(jnp.bfloat16)


def phase_backward(hidden, gain_pair, coords, weight, grad_out):

    def local_mix(state_rows, gain_values):
        return mixing(state_rows, gain_values, coords)

    mixed_rows, pullback = jax.vjp(local_mix, hidden, gain_pair)
    weight_term = lax.dot_general(
        mixed_rows, grad_out, (((0,), (0,)), ((), ())), preferred_element_type=jnp.float32
    )
    grad_mixed = lax.dot_general(
        grad_out, weight, (((1,), (1,)), ((), ())), preferred_element_type=jnp.float32
    ).astype(jnp.bfloat16)
    grad_hidden, gain_term = pullback(grad_mixed)
    grad_in = (grad_out.astype(jnp.float32) + grad_hidden.astype(jnp.float32)).astype(jnp.bfloat16)
    return (grad_in, weight_term, gain_term)


def shards(clips, positions, out_proj, qk_gains, cotangent):
    depth = lax.axis_size("pipe")
    place = lax.axis_index("pipe")
    mirror = depth - 1 - place
    micro_count = clips.shape[1]
    bit_count = depth.bit_length() - 1
    far_weight = out_proj[0]
    far_gains = qk_gains[0]
    for bit_index in range(bit_count):
        far_weight, far_gains = from_partner((far_weight, far_gains), "pipe", bit_index)
    near_full, far_full = (
        lax.all_gather(out_proj[0], "dp", axis=0, tiled=True),
        lax.all_gather(far_weight, "dp", axis=0, tiled=True),
    )
    near_pair = qk_gains[0].astype(jnp.float32)
    far_pair = far_gains.astype(jnp.float32)
    tick_count = depth + micro_count - 1
    zero_rows = jnp.zeros(clips.shape[2:], jnp.bfloat16)

    def slot_state(slot_value):
        live_slot = (slot_value >= 0) & (slot_value < micro_count)
        return (live_slot, jnp.clip(slot_value, 0, micro_count - 1))

    def forward_inputs(tick_index, carry):
        received_near, received_far, store_near, store_far = carry
        live_near, clip_near = slot_state(tick_index - place)
        live_far, clip_far = slot_state(tick_index - mirror)
        input_near = jnp.where(place == 0, clips[0, clip_near], received_near)
        input_far = jnp.where(place == depth - 1, clips[1, clip_far], received_far)
        store_near = store_near.at[clip_near].set(
            jnp.where(live_near, input_near, store_near[clip_near])
        )
        store_far = store_far.at[clip_far].set(jnp.where(live_far, input_far, store_far[clip_far]))
        return (
            (live_near, clip_near, input_near),
            (live_far, clip_far, input_far),
            store_near,
            store_far,
        )

    def forward_tick(carry, tick_index):
        near_info, far_info, store_near, store_far = forward_inputs(tick_index, carry)
        live_near, clip_near, input_near = near_info
        live_far, clip_far, input_far = far_info
        output_near = lax.cond(
            live_near,
            lambda: phase_forward(input_near, near_pair, positions[:, 0, clip_near], near_full),
            lambda: zero_rows,
        )
        output_far = lax.cond(
            live_far,
            lambda: phase_forward(input_far, far_pair, positions[:, 1, clip_far], far_full),
            lambda: zero_rows,
        )
        next_near = shifted(output_near, "pipe", 1)
        next_far = shifted(output_far, "pipe", -1)
        return ((next_near, next_far, store_near, store_far), None)

    empty_store = jnp.zeros((micro_count,) + clips.shape[2:], jnp.bfloat16)
    carry, unused = lax.scan(
        forward_tick, (zero_rows, zero_rows, empty_store, empty_store), jnp.arange(tick_count - 1)
    )
    unused_near, unused_far, store_near, store_far = forward_inputs(tick_count - 1, carry)

    def backward_phase(tick_index, carry):
        received_near, received_far, sum_near, sum_far, gain_near, gain_far = carry
        live_near, clip_near = slot_state(tick_index - mirror)
        live_far, clip_far = slot_state(tick_index - place)
        incoming_near = jnp.where(place == depth - 1, cotangent[0, clip_near], received_near)
        incoming_far = jnp.where(place == 0, cotangent[1, clip_far], received_far)

        def work_near():
            grad_in, weight_term, gain_term = phase_backward(
                store_near[clip_near],
                near_pair,
                positions[:, 0, clip_near],
                near_full,
                incoming_near,
            )
            return (grad_in, sum_near + weight_term, gain_near + gain_term)

        def skip_near():
            return (zero_rows, sum_near, gain_near)

        def work_far():
            grad_in, weight_term, gain_term = phase_backward(
                store_far[clip_far], far_pair, positions[:, 1, clip_far], far_full, incoming_far
            )
            return (grad_in, sum_far + weight_term, gain_far + gain_term)

        def skip_far():
            return (zero_rows, sum_far, gain_far)

        grad_near, sum_near, gain_near = lax.cond(live_near, work_near, skip_near)
        grad_far, sum_far, gain_far = lax.cond(live_far, work_far, skip_far)
        return (grad_near, grad_far, sum_near, sum_far, gain_near, gain_far)

    def backward_tick(carry, tick_index):
        grad_near, grad_far, sum_near, sum_far, gain_near, gain_far = backward_phase(
            tick_index, carry
        )
        next_near = shifted(grad_near, "pipe", -1)
        next_far = shifted(grad_far, "pipe", 1)
        return ((next_near, next_far, sum_near, sum_far, gain_near, gain_far), None)

    channels = clips.shape[3]
    zero_square = jnp.zeros((channels, channels), jnp.float32)
    zero_gains = jnp.zeros(near_pair.shape, jnp.float32)
    start_carry = (zero_rows, zero_rows, zero_square, zero_square, zero_gains, zero_gains)
    carry, unused = lax.scan(backward_tick, start_carry, jnp.arange(tick_count - 1))
    unused_near, unused_far, sum_near, sum_far, gain_near, gain_far = backward_phase(
        tick_count - 1, carry
    )
    near_shard, far_shard = (
        lax.psum_scatter(
            sum_near.astype(jnp.bfloat16), "dp", scatter_dimension=0, tiled=True
        ).astype(jnp.float32),
        lax.psum_scatter(
            sum_far.astype(jnp.bfloat16), "dp", scatter_dimension=0, tiled=True
        ).astype(jnp.float32),
    )
    near_gain_sum, far_gain_sum = lax.psum((gain_near, gain_far), "dp")
    for bit_index in range(bit_count):
        far_shard, far_gain_sum = (
            from_partner(far_shard.astype(jnp.bfloat16), "pipe", bit_index).astype(far_shard.dtype),
            from_partner(far_gain_sum.astype(jnp.bfloat16), "pipe", bit_index).astype(
                far_gain_sum.dtype
            ),
        )
    shard_total = near_shard + far_shard
    gains_total = near_gain_sum + far_gain_sum
    return (shard_total[None], gains_total[None])


def solution(mesh):
    placed = (
        P(None, None, "dp", None),
        P(None, None, None, "dp"),
        P("pipe", "dp", None),
        P("pipe", None, None),
        P(None, None, "dp", None),
    )
    return jax.shard_map(
        shards,
        mesh=mesh,
        in_specs=placed,
        out_specs=(P("pipe", "dp", None), P("pipe", None, None)),
        check_vma=False,
    )
```

profile of v0, /device:TPU:0, one launch (start us, length us, event | category | flops | bytes accessed | tf_op | source)
XLA Modules:
  0.0 1719.9 jit_solution(15197609900141042503)
XLA Ops:
  9.6 7.2 collective-permute-done.7
  18.7 6.2 collective-permute-done.8
  28.2 5.6 collective-permute-done.9
  52.8 17.3 %all-gather.6.cloned.1.call-done = bf16[1,1536,1536]{2,1,0:T(8,128)(2,1)} async-done(((bf16[1,96,1536]{2,1,0:T(8,128)(2,1)}), bf16[1,1536,1536]{2,1,0:T(8,128)(2,1)}) %all-gather.6.cloned.1.call-update) | async-done | bytes 4718608 | tf_op jit(solution)/shard_map/all_gather | solution.py:96
  70.1 57.3 %all-gather.4.cloned.1.call-done = bf16[1536,1536]{1,0:T(8,128)(2,1)} async-done(((bf16[96,1536]{1,0:T(8,128)(2,1)}), bf16[1536,1536]{1,0:T(8,128)(2,1)}) %all-gather.4.cloned.1.call-update) | async-done | bytes 4718608 | tf_op jit(solution)/shard_map/all_gather | solution.py:97
  130.6 506.6 %while.42 = (s32[]{:T(128)}, bf16[128,1536]{1,0:T(8,128)(2,1)S(1)}, bf16[128,1536]{1,0:T(8,128)(2,1)}, bf16[3,128,1536]{1,2,0:T(8,128)(2,1)}, bf16[3,128,1536]{1...) while((s32[]{:T(128)}, bf16[128,1536]{1,0:T(8,128)(2,1)S(1)}, ...), condition=%wide.region_11.12_spmd, body=%wide.region_0.11_spmd.sunk | while | flops 1921670144 | bytes 62277136 | solution.py:144
  141.6 28.7 %conditional.12 = (bf16[128,1536]{1,0:T(8,128)(2,1)}) conditional(s32[]{:T(128)} %convert_element_type.772, () %tuple.355, (bf16[128,1536]{1,0:T(8,128)(2,1)S(1)}, f32[2,128]{1,0:T(2,128)}, s32[]{:T(128)}, s32[3,2,3,128]{3,2,1,0:T(4,128)}, bf16[1536,1536]{1,0:T(8,128)(2,1)}) %tuple.356), branch_computations={%region_1.1_spmd, %region_2.4_spmd} | conditional | flops 960245248 | bytes 24682602 | solution.py:129
  152.0 4.4 concatenate.50
  175.0 5.9 collective-permute-done
  191.7 28.7 %conditional.12 = (bf16[128,1536]{1,0:T(8,128)(2,1)}) conditional(s32[]{:T(128)} %convert_element_type.772, () %tuple.355, (bf16[128,1536]{1,0:T(8,128)(2,1)S(1)}, f32[2,128]{1,0:T(2,128)}, s32[]{:T(128)}, s32[3,2,3,128]{3,2,1,0:T(4,128)}, bf16[1536,1536]{1,0:T(8,128)(2,1)}) %tuple.356), branch_computations={%region_1.1_spmd, %region_2.4_spmd} | conditional | flops 960245248 | bytes 24682602 | solution.py:129
  202.1 4.4 concatenate.50
  220.4 4.9 collective-permute-start
  228.7 5.1 collective-permute-done
  244.5 28.7 %conditional.12 = (bf16[128,1536]{1,0:T(8,128)(2,1)}) conditional(s32[]{:T(128)} %convert_element_type.772, () %tuple.355, (bf16[128,1536]{1,0:T(8,128)(2,1)S(1)}, f32[2,128]{1,0:T(2,128)}, s32[]{:T(128)}, s32[3,2,3,128]{3,2,1,0:T(4,128)}, bf16[1536,1536]{1,0:T(8,128)(2,1)}) %tuple.356), branch_computations={%region_1.1_spmd, %region_2.4_spmd} | conditional | flops 960245248 | bytes 24682602 | solution.py:129
  255.0 4.4 concatenate.50
  273.2 4.9 collective-permute-start
  297.3 33.1 %collective-permute-start = (bf16[128,1536]{1,0:T(8,128)(2,1)}, bf16[128,1536]{1,0:T(8,128)(2,1)S(1)}, u32[]{:S(2)}, u32[]{:S(2)}) collective-permute-start(bf16[128,1536]{1,0:T(8,128)(2,1)} %get-tuple-element.1727), channel_id=1, source_target_pairs={{0,16},{16,32},{32,48},{48,64},{64,80},{80,96},{96,112},{1,17},{17... | collective-permute-start | bytes 1179656 | tf_op jit(solution)/shard_map/while/body/eval_jaxpr/ppermute | solution.py:16
  348.5 5.8 collective-permute-start
  371.5 33.7 %collective-permute-start = (bf16[128,1536]{1,0:T(8,128)(2,1)}, bf16[128,1536]{1,0:T(8,128)(2,1)S(1)}, u32[]{:S(2)}, u32[]{:S(2)}) collective-permute-start(bf16[128,1536]{1,0:T(8,128)(2,1)} %get-tuple-element.1727), channel_id=1, source_target_pairs={{0,16},{16,32},{32,48},{48,64},{64,80},{80,96},{96,112},{1,17},{17... | collective-permute-start | bytes 1179656 | tf_op jit(solution)/shard_map/while/body/eval_jaxpr/ppermute | solution.py:16
  422.3 79.9 %collective-permute-start = (bf16[128,1536]{1,0:T(8,128)(2,1)}, bf16[128,1536]{1,0:T(8,128)(2,1)S(1)}, u32[]{:S(2)}, u32[]{:S(2)}) collective-permute-start(bf16[128,1536]{1,0:T(8,128)(2,1)} %get-tuple-element.1727), channel_id=1, source_target_pairs={{0,16},{16,32},{32,48},{48,64},{64,80},{80,96},{96,112},{1,17},{17... | collective-permute-start | bytes 1179656 | tf_op jit(solution)/shard_map/while/body/eval_jaxpr/ppermute | solution.py:16
  516.4 26.3 %conditional.13 = (bf16[128,1536]{1,0:T(8,128)(2,1)}) conditional(s32[]{:T(128)} %convert_element_type.773, () %tuple.357, (bf16[128,1536]{1,0:T(8,128)(2,1)S(1)}, f32[2,128]{1,0:T(2,128)}, s32[]{:T(128)}, s32[3,2,3,128]{3,2,1,0:T(4,128)}, bf16[1536,1536]{1,0:T(8,128)(2,1)}) %tuple.358), branch_computations={%region_5.5_spmd, %region_6.0_spmd} | conditional | flops 960245248 | bytes 24223626 | solution.py:134
  524.3 4.4 concatenate.52
  544.9 34.6 %collective-permute-start = (bf16[128,1536]{1,0:T(8,128)(2,1)}, bf16[128,1536]{1,0:T(8,128)(2,1)S(1)}, u32[]{:S(2)}, u32[]{:S(2)}) collective-permute-start(bf16[128,1536]{1,0:T(8,128)(2,1)} %get-tuple-element.1727), channel_id=1, source_target_pairs={{0,16},{16,32},{32,48},{48,64},{64,80},{80,96},{96,112},{1,17},{17... | collective-permute-start | bytes 1179656 | tf_op jit(solution)/shard_map/while/body/eval_jaxpr/ppermute | solution.py:16
  595.0 26.3 %conditional.13 = (bf16[128,1536]{1,0:T(8,128)(2,1)}) conditional(s32[]{:T(128)} %convert_element_type.773, () %tuple.357, (bf16[128,1536]{1,0:T(8,128)(2,1)S(1)}, f32[2,128]{1,0:T(2,128)}, s32[]{:T(128)}, s32[3,2,3,128]{3,2,1,0:T(4,128)}, bf16[1536,1536]{1,0:T(8,128)(2,1)}) %tuple.358), branch_computations={%region_5.5_spmd, %region_6.0_spmd} | conditional | flops 960245248 | bytes 24223626 | solution.py:134
  602.8 4.4 concatenate.52
  623.4 7.0 collective-permute-start
  647.6 4.7 broadcast_in_dim.127.clone
  652.4 4.9 broadcast_in_dim.127
  657.3 771.0 %while.43 = (s32[]{:T(128)}, bf16[128,1536]{0,1:T(8,128)(2,1)}, bf16[128,1536]{0,1:T(8,128)(2,1)}, f32[1536,1536]{1,0:T(8,128)}, f32[1536,1536]{1,0:T(8,128)}, /...) while((s32[]{:T(128)}, bf16[128,1536]{0,1:T(8,128)(2,1)}, ...), condition=%wide.region_31.32_spmd, body=%wide.region_14.31_spmd.sunk | while | flops 4563310592 | bytes 155919184 | solution.py:194
  684.9 50.8 %conditional.15 = (bf16[128,1536]{0,1:T(8,128)(2,1)}, f32[1536,1536]{1,0:T(8,128)}, f32[2,128]{1,0:T(2,128)}) conditional(s32[]{:T(128)} %convert_element_type.775, (f32[1536,1536]{1,0:T(8,128)}, f32[2,128]{1,0:T(2,128)}) %tuple.362, (pred[]{:T(512)}, s32[]{:T(128)}, bf16[2,3,128,1536]{2,3,1,0:T(8,128)(2,1)}, bf16[128,1536]{0,1:T(8,128)(2,1)}, ...), branch_computations={%region_23.23_spmd, %region_24.30_spmd} | conditional | flops 2281655296 | bytes 75604112 | solution.py:179
  700.0 4.4 concatenate.59
  727.0 8.6 convolution_add_fusion.3
  737.0 5.6 collective-permute-done.3
  748.1 50.8 %conditional.15 = (bf16[128,1536]{0,1:T(8,128)(2,1)}, f32[1536,1536]{1,0:T(8,128)}, f32[2,128]{1,0:T(2,128)}) conditional(s32[]{:T(128)} %convert_element_type.775, (f32[1536,1536]{1,0:T(8,128)}, f32[2,128]{1,0:T(2,128)}) %tuple.362, (pred[]{:T(512)}, s32[]{:T(128)}, bf16[2,3,128,1536]{2,3,1,0:T(8,128)(2,1)}, bf16[128,1536]{0,1:T(8,128)(2,1)}, ...), branch_computations={%region_23.23_spmd, %region_24.30_spmd} | conditional | flops 2281655296 | bytes 75604112 | solution.py:179
  790.3 8.6 convolution_add_fusion.3
  798.9 5.0 collective-permute-start.3
  804.0 5.6 collective-permute-done.3
  815.1 50.8 %conditional.15 = (bf16[128,1536]{0,1:T(8,128)(2,1)}, f32[1536,1536]{1,0:T(8,128)}, f32[2,128]{1,0:T(2,128)}) conditional(s32[]{:T(128)} %convert_element_type.775, (f32[1536,1536]{1,0:T(8,128)}, f32[2,128]{1,0:T(2,128)}) %tuple.362, (pred[]{:T(512)}, s32[]{:T(128)}, bf16[2,3,128,1536]{2,3,1,0:T(8,128)(2,1)}, bf16[128,1536]{0,1:T(8,128)(2,1)}, ...), branch_computations={%region_23.23_spmd, %region_24.30_spmd} | conditional | flops 2281655296 | bytes 75604112 | solution.py:179
  857.2 8.6 convolution_add_fusion.3
  865.9 5.0 collective-permute-start.3
  870.9 5.6 collective-permute-done.3
  882.8 58.1 %collective-permute-start.3 = (bf16[128,1536]{0,1:T(8,128)(2,1)}, bf16[128,1536]{0,1:T(8,128)(2,1)S(1)}, u32[]{:S(2)}, u32[]{:S(2)}) collective-permute-start(bf16[128,1536]{0,1:T(8,128)(2,1)} %get-tuple-element.1565), channel_id=1, source_target_pairs={{0,16},{16,32},{32,48},{48,64},{64,80},{80,96},{96,112},{1,17},{17... | collective-permute-start | bytes 1179656 | tf_op jit(solution)/shard_map/while/body/eval_jaxpr/ppermute | solution.py:16
  940.9 5.6 collective-permute-done.3
  952.8 8.1 collective-permute-start.3
  972.8 55.9 %collective-permute-start.3 = (bf16[128,1536]{0,1:T(8,128)(2,1)}, bf16[128,1536]{0,1:T(8,128)(2,1)S(1)}, u32[]{:S(2)}, u32[]{:S(2)}) collective-permute-start(bf16[128,1536]{0,1:T(8,128)(2,1)} %get-tuple-element.1565), channel_id=1, source_target_pairs={{0,16},{16,32},{32,48},{48,64},{64,80},{80,96},{96,112},{1,17},{17... | collective-permute-start | bytes 1179656 | tf_op jit(solution)/shard_map/while/body/eval_jaxpr/ppermute | solution.py:16
  1040.7 189.2 %collective-permute-start.3 = (bf16[128,1536]{0,1:T(8,128)(2,1)}, bf16[128,1536]{0,1:T(8,128)(2,1)S(1)}, u32[]{:S(2)}, u32[]{:S(2)}) collective-permute-start(bf16[128,1536]{0,1:T(8,128)(2,1)} %get-tuple-element.1565), channel_id=1, source_target_pairs={{0,16},{16,32},{32,48},{48,64},{64,80},{80,96},{96,112},{1,17},{17... | collective-permute-start | bytes 1179656 | tf_op jit(solution)/shard_map/while/body/eval_jaxpr/ppermute | solution.py:16
  1238.2 52.3 %conditional.14 = (bf16[128,1536]{0,1:T(8,128)(2,1)}, f32[1536,1536]{1,0:T(8,128)}, f32[2,128]{1,0:T(2,128)}) conditional(s32[]{:T(128)} %convert_element_type.774, (f32[1536,1536]{1,0:T(8,128)}, f32[2,128]{1,0:T(2,128)}) %tuple.360, (pred[]{:T(512)}, s32[]{:T(128)}, bf16[2,3,128,1536]{2,3,1,0:T(8,128)(2,1)}, bf16[128,1536]{0,1:T(8,128)(2,1)}, ...), branch_computations={%region_15.15_spmd, %region_16.22_spmd} | conditional | flops 2281655296 | bytes 75595864 | solution.py:178
  1281.7 8.8 convolution_add_fusion.2
  1293.3 56.0 %collective-permute-start.3 = (bf16[128,1536]{0,1:T(8,128)(2,1)}, bf16[128,1536]{0,1:T(8,128)(2,1)S(1)}, u32[]{:S(2)}, u32[]{:S(2)}) collective-permute-start(bf16[128,1536]{0,1:T(8,128)(2,1)} %get-tuple-element.1565), channel_id=1, source_target_pairs={{0,16},{16,32},{32,48},{48,64},{64,80},{80,96},{96,112},{1,17},{17... | collective-permute-start | bytes 1179656 | tf_op jit(solution)/shard_map/while/body/eval_jaxpr/ppermute | solution.py:16
  1357.5 52.3 %conditional.14 = (bf16[128,1536]{0,1:T(8,128)(2,1)}, f32[1536,1536]{1,0:T(8,128)}, f32[2,128]{1,0:T(2,128)}) conditional(s32[]{:T(128)} %convert_element_type.774, (f32[1536,1536]{1,0:T(8,128)}, f32[2,128]{1,0:T(2,128)}) %tuple.360, (pred[]{:T(512)}, s32[]{:T(128)}, bf16[2,3,128,1536]{2,3,1,0:T(8,128)(2,1)}, bf16[128,1536]{0,1:T(8,128)(2,1)}, ...), branch_computations={%region_15.15_spmd, %region_16.22_spmd} | conditional | flops 2281655296 | bytes 75595864 | solution.py:178
  1401.1 8.8 convolution_add_fusion.2
  1412.6 5.8 collective-permute-start.3
  1428.3 12.3 conditional.7
  1440.5 6.4 convert_element_type.520
  1447.7 51.6 %conditional.6 = ((f32[1536,1536]{1,0:T(8,128)}, f32[2,128]{1,0:T(2,128)})) conditional(s32[]{:T(128)} %convert_element_type.514, (f32[1536,1536]{1,0:T(8,128)}, f32[2,128]{1,0:T(2,128)}) %tuple.96, (s32[]{:T(128)}, bf16[3,128,1536]{1,2,0:T(8,128)(2,1)}, f32[2,128]{1,0:T(2,128)}, s32[3,2,3,128]{3,1,2,0:T(2,128)S(1)}, pred[]{:T(512)}, ...), branch_computations={%region_32.33_spmd, %region_33.39_spmd} | conditional | flops 2227777280 | bytes 66656552 | solution.py:178
  1463.4 4.7 concatenate.61
  1483.7 9.0 convolution_add_fusion.4
  1499.3 6.5 convert_element_type.517
  1505.8 119.3 %reduce-scatter.5.cloned.1.call-done = bf16[96,1536]{1,0:T(8,128)(2,1)} async-done(((bf16[1536,1536]{1,0:T(8,128)(2,1)}), bf16[96,1536]{1,0:T(8,128)(2,1)}) %reduce-scatter.5.cloned.1.call-update) | async-done | bytes 294928 | tf_op jit(solution)/shard_map/reduce_scatter | solution.py:202
  1625.7 6.9 collective-permute-done.10
  1634.1 5.2 collective-permute-done.11
  1642.8 33.8 %all-reduce.80 = (f32[2,128]{1,0:T(2,128)S(1)}, bf16[2,128]{1,0:T(2,128)(2,1)S(1)}) all-reduce(f32[2,128]{1,0:T(2,128)} %get-tuple-element.740, f32[2,128]{1,0:T(2,128)S(1)} %copy-done.64), channel_id=1, replica_groups=mesh['pipe'=8,'dp'=16] {'dp'}, use_global_device_ids=true, to_apply=%region_48.49 | all-reduce | flops 512 | bytes 3584 | tf_op jit(solution)/shard_map/psum | solution.py:206
  1684.3 4.6 collective-permute-done.15
  1689.5 21.5 %reduce-scatter.3.cloned.1.call-done = bf16[96,1536]{1,0:T(8,128)(2,1)} async-done(((bf16[1536,1536]{1,0:T(8,128)(2,1)}), bf16[96,1536]{1,0:T(8,128)(2,1)}) %reduce-scatter.3.cloned.1.call-update) | async-done | bytes 294928 | tf_op jit(solution)/shard_map/reduce_scatter | solution.py:199
  (806 shorter events, 648.8 us)
Async XLA Ops:
  7.2 42.6 %copy-start.19 = (bf16[2,3,128,1536]{3,2,1,0:T(8,128)(2,1)S(1)}, bf16[2,3,128,1536]{3,2,1,0:T(8,128)(2,1)}, u32[]{:S(2)}) copy-start(bf16[2,3,128,1536]{3,2,1,0:T(8,128)(2,1)} %param.33) | copy-start | bytes 7077892
  7.2 62.9 %all-gather.6.cloned.1.call-start = ((), (), s32[]{:S(2)}) async-start(), calls=%async_computation.5 | async-start | bytes 5013504 | tf_op jit(solution)/shard_map/all_gather | solution.py:96
  7.9 119.5 %all-gather.4.cloned.1.call-start = ((), (), s32[]{:S(2)}) async-start(), calls=%async_computation.2 | async-start | bytes 5013504 | tf_op jit(solution)/shard_map/all_gather | solution.py:97
  8.0 8.9 collective-permute-start.7
  16.9 8.0 collective-permute-start.8
  24.8 8.9 collective-permute-start.9
  34.5 1590.6 %reduce-scatter.5.cloned.1.call-start = ((), (), s32[]{:S(2)}) async-start(), calls=%async_computation.4 | async-start | bytes 5013504 | tf_op jit(solution)/shard_map/reduce_scatter | solution.py:202
  34.6 5.5 collective-permute-start.4
  40.0 3.6 collective-permute-start.5
  43.6 8.6 collective-permute-start.6
  47.9 82.7 %copy-start.65 = (s32[3]{0:T(128)S(1)}, s32[3]{0:T(128)}, u32[]{:S(2)}) copy-start(s32[3]{0:T(128)} %constant.437.clone.1) | copy-start | bytes 40
  140.3 34.7 %collective-permute-start.1 = (bf16[128,1536]{1,0:T(8,128)(2,1)}, bf16[128,1536]{1,0:T(8,128)(2,1)}, u32[]{:S(2)}, u32[]{:S(2)}) collective-permute-start(bf16[128,1536]{1,0:T(8,128)(2,1)} %get-tuple-element.1728), channel_id=1, source_target_pairs={{16,0},{32,16},{48,32},{64,48},{80,64},{96,80},{112,96},{17,1},{33... | collective-permute-start | bytes 1179656 | tf_op jit(solution)/shard_map/while/body/eval_jaxpr/ppermute | solution.py:16
  170.3 10.7 collective-permute-start
  190.4 38.3 %collective-permute-start.1 = (bf16[128,1536]{1,0:T(8,128)(2,1)}, bf16[128,1536]{1,0:T(8,128)(2,1)}, u32[]{:S(2)}, u32[]{:S(2)}) collective-permute-start(bf16[128,1536]{1,0:T(8,128)(2,1)} %get-tuple-element.1728), channel_id=1, source_target_pairs={{16,0},{32,16},{48,32},{64,48},{80,64},{96,80},{112,96},{17,1},{33... | collective-permute-start | bytes 1179656 | tf_op jit(solution)/shard_map/while/body/eval_jaxpr/ppermute | solution.py:16
  220.4 13.4 collective-permute-start
  243.2 38.3 %collective-permute-start.1 = (bf16[128,1536]{1,0:T(8,128)(2,1)}, bf16[128,1536]{1,0:T(8,128)(2,1)}, u32[]{:S(2)}, u32[]{:S(2)}) collective-permute-start(bf16[128,1536]{1,0:T(8,128)(2,1)} %get-tuple-element.1728), channel_id=1, source_target_pairs={{16,0},{32,16},{48,32},{64,48},{80,64},{96,80},{112,96},{17,1},{33... | collective-permute-start | bytes 1179656 | tf_op jit(solution)/shard_map/while/body/eval_jaxpr/ppermute | solution.py:16
  273.2 12.6 collective-permute-start
  295.2 38.6 %collective-permute-start.1 = (bf16[128,1536]{1,0:T(8,128)(2,1)}, bf16[128,1536]{1,0:T(8,128)(2,1)}, u32[]{:S(2)}, u32[]{:S(2)}) collective-permute-start(bf16[128,1536]{1,0:T(8,128)(2,1)} %get-tuple-element.1728), channel_id=1, source_target_pairs={{16,0},{32,16},{48,32},{64,48},{80,64},{96,80},{112,96},{17,1},{33... | collective-permute-start | bytes 1179656 | tf_op jit(solution)/shard_map/while/body/eval_jaxpr/ppermute | solution.py:16
  297.3 39.6 %collective-permute-start = (bf16[128,1536]{1,0:T(8,128)(2,1)}, bf16[128,1536]{1,0:T(8,128)(2,1)S(1)}, u32[]{:S(2)}, u32[]{:S(2)}) collective-permute-start(bf16[128,1536]{1,0:T(8,128)(2,1)} %get-tuple-element.1727), channel_id=1, source_target_pairs={{0,16},{16,32},{32,48},{48,64},{64,80},{80,96},{96,112},{1,17},{17... | collective-permute-start | bytes 1179656 | tf_op jit(solution)/shard_map/while/body/eval_jaxpr/ppermute | solution.py:16
  346.4 11.6 collective-permute-start.1
  348.5 11.5 collective-permute-start
  369.4 39.2 %collective-permute-start.1 = (bf16[128,1536]{1,0:T(8,128)(2,1)}, bf16[128,1536]{1,0:T(8,128)(2,1)}, u32[]{:S(2)}, u32[]{:S(2)}) collective-permute-start(bf16[128,1536]{1,0:T(8,128)(2,1)} %get-tuple-element.1728), channel_id=1, source_target_pairs={{16,0},{32,16},{48,32},{64,48},{80,64},{96,80},{112,96},{17,1},{33... | collective-permute-start | bytes 1179656 | tf_op jit(solution)/shard_map/while/body/eval_jaxpr/ppermute | solution.py:16
  371.5 39.3 %collective-permute-start = (bf16[128,1536]{1,0:T(8,128)(2,1)}, bf16[128,1536]{1,0:T(8,128)(2,1)S(1)}, u32[]{:S(2)}, u32[]{:S(2)}) collective-permute-start(bf16[128,1536]{1,0:T(8,128)(2,1)} %get-tuple-element.1727), channel_id=1, source_target_pairs={{0,16},{16,32},{32,48},{48,64},{64,80},{80,96},{96,112},{1,17},{17... | collective-permute-start | bytes 1179656 | tf_op jit(solution)/shard_map/while/body/eval_jaxpr/ppermute | solution.py:16
  420.2 85.4 %collective-permute-start.1 = (bf16[128,1536]{1,0:T(8,128)(2,1)}, bf16[128,1536]{1,0:T(8,128)(2,1)}, u32[]{:S(2)}, u32[]{:S(2)}) collective-permute-start(bf16[128,1536]{1,0:T(8,128)(2,1)} %get-tuple-element.1728), channel_id=1, source_target_pairs={{16,0},{32,16},{48,32},{64,48},{80,64},{96,80},{112,96},{17,1},{33... | collective-permute-start | bytes 1179656 | tf_op jit(solution)/shard_map/while/body/eval_jaxpr/ppermute | solution.py:16
  422.3 85.5 %collective-permute-start = (bf16[128,1536]{1,0:T(8,128)(2,1)}, bf16[128,1536]{1,0:T(8,128)(2,1)S(1)}, u32[]{:S(2)}, u32[]{:S(2)}) collective-permute-start(bf16[128,1536]{1,0:T(8,128)(2,1)} %get-tuple-element.1727), channel_id=1, source_target_pairs={{0,16},{16,32},{32,48},{48,64},{64,80},{80,96},{96,112},{1,17},{17... | collective-permute-start | bytes 1179656 | tf_op jit(solution)/shard_map/while/body/eval_jaxpr/ppermute | solution.py:16
  542.8 43.6 %collective-permute-start.1 = (bf16[128,1536]{1,0:T(8,128)(2,1)}, bf16[128,1536]{1,0:T(8,128)(2,1)}, u32[]{:S(2)}, u32[]{:S(2)}) collective-permute-start(bf16[128,1536]{1,0:T(8,128)(2,1)} %get-tuple-element.1728), channel_id=1, source_target_pairs={{16,0},{32,16},{48,32},{64,48},{80,64},{96,80},{112,96},{17,1},{33... | collective-permute-start | bytes 1179656 | tf_op jit(solution)/shard_map/while/body/eval_jaxpr/ppermute | solution.py:16
  544.9 41.5 %collective-permute-start = (bf16[128,1536]{1,0:T(8,128)(2,1)}, bf16[128,1536]{1,0:T(8,128)(2,1)S(1)}, u32[]{:S(2)}, u32[]{:S(2)}) collective-permute-start(bf16[128,1536]{1,0:T(8,128)(2,1)} %get-tuple-element.1727), channel_id=1, source_target_pairs={{0,16},{16,32},{32,48},{48,64},{64,80},{80,96},{96,112},{1,17},{17... | collective-permute-start | bytes 1179656 | tf_op jit(solution)/shard_map/while/body/eval_jaxpr/ppermute | solution.py:16
  621.3 15.8 collective-permute-start.1
  623.4 13.7 collective-permute-start
  682.9 54.1 %collective-permute-start.2 = (bf16[128,1536]{0,1:T(8,128)(2,1)}, bf16[128,1536]{0,1:T(8,128)(2,1)}, u32[]{:S(2)}, u32[]{:S(2)}) collective-permute-start(bf16[128,1536]{0,1:T(8,128)(2,1)} %get-tuple-element.1564), channel_id=1, source_target_pairs={{16,0},{32,16},{48,32},{64,48},{80,64},{96,80},{112,96},{17,1},{33... | collective-permute-start | bytes 1179656 | tf_op jit(solution)/shard_map/while/body/eval_jaxpr/ppermute | solution.py:16
  725.4 10.3 copy-start.61
  735.7 6.9 collective-permute-start.3
  746.1 57.8 %collective-permute-start.2 = (bf16[128,1536]{0,1:T(8,128)(2,1)}, bf16[128,1536]{0,1:T(8,128)(2,1)}, u32[]{:S(2)}, u32[]{:S(2)}) collective-permute-start(bf16[128,1536]{0,1:T(8,128)(2,1)} %get-tuple-element.1564), channel_id=1, source_target_pairs={{16,0},{32,16},{48,32},{64,48},{80,64},{96,80},{112,96},{17,1},{33... | collective-permute-start | bytes 1179656 | tf_op jit(solution)/shard_map/while/body/eval_jaxpr/ppermute | solution.py:16
  788.6 10.3 copy-start.61
  798.9 10.6 collective-permute-start.3
  813.1 57.8 %collective-permute-start.2 = (bf16[128,1536]{0,1:T(8,128)(2,1)}, bf16[128,1536]{0,1:T(8,128)(2,1)}, u32[]{:S(2)}, u32[]{:S(2)}) collective-permute-start(bf16[128,1536]{0,1:T(8,128)(2,1)} %get-tuple-element.1564), channel_id=1, source_target_pairs={{16,0},{32,16},{48,32},{64,48},{80,64},{96,80},{112,96},{17,1},{33... | collective-permute-start | bytes 1179656 | tf_op jit(solution)/shard_map/while/body/eval_jaxpr/ppermute | solution.py:16
  855.5 10.3 copy-start.61
  865.9 10.6 collective-permute-start.3
  880.0 60.9 %collective-permute-start.2 = (bf16[128,1536]{0,1:T(8,128)(2,1)}, bf16[128,1536]{0,1:T(8,128)(2,1)}, u32[]{:S(2)}, u32[]{:S(2)}) collective-permute-start(bf16[128,1536]{0,1:T(8,128)(2,1)} %get-tuple-element.1564), channel_id=1, source_target_pairs={{16,0},{32,16},{48,32},{64,48},{80,64},{96,80},{112,96},{17,1},{33... | collective-permute-start | bytes 1179656 | tf_op jit(solution)/shard_map/while/body/eval_jaxpr/ppermute | solution.py:16
  882.8 63.6 %collective-permute-start.3 = (bf16[128,1536]{0,1:T(8,128)(2,1)}, bf16[128,1536]{0,1:T(8,128)(2,1)S(1)}, u32[]{:S(2)}, u32[]{:S(2)}) collective-permute-start(bf16[128,1536]{0,1:T(8,128)(2,1)} %get-tuple-element.1565), channel_id=1, source_target_pairs={{0,16},{16,32},{32,48},{48,64},{64,80},{80,96},{96,112},{1,17},{17... | collective-permute-start | bytes 1179656 | tf_op jit(solution)/shard_map/while/body/eval_jaxpr/ppermute | solution.py:16
  950.0 13.5 collective-permute-start.2
  952.8 13.7 collective-permute-start.3
  970.0 61.3 %collective-permute-start.2 = (bf16[128,1536]{0,1:T(8,128)(2,1)}, bf16[128,1536]{0,1:T(8,128)(2,1)}, u32[]{:S(2)}, u32[]{:S(2)}) collective-permute-start(bf16[128,1536]{0,1:T(8,128)(2,1)} %get-tuple-element.1564), channel_id=1, source_target_pairs={{16,0},{32,16},{48,32},{64,48},{80,64},{96,80},{112,96},{17,1},{33... | collective-permute-start | bytes 1179656 | tf_op jit(solution)/shard_map/while/body/eval_jaxpr/ppermute | solution.py:16
  972.8 61.5 %collective-permute-start.3 = (bf16[128,1536]{0,1:T(8,128)(2,1)}, bf16[128,1536]{0,1:T(8,128)(2,1)S(1)}, u32[]{:S(2)}, u32[]{:S(2)}) collective-permute-start(bf16[128,1536]{0,1:T(8,128)(2,1)} %get-tuple-element.1565), channel_id=1, source_target_pairs={{0,16},{16,32},{32,48},{48,64},{64,80},{80,96},{96,112},{1,17},{17... | collective-permute-start | bytes 1179656 | tf_op jit(solution)/shard_map/while/body/eval_jaxpr/ppermute | solution.py:16
  1037.9 194.6 %collective-permute-start.2 = (bf16[128,1536]{0,1:T(8,128)(2,1)}, bf16[128,1536]{0,1:T(8,128)(2,1)}, u32[]{:S(2)}, u32[]{:S(2)}) collective-permute-start(bf16[128,1536]{0,1:T(8,128)(2,1)} %get-tuple-element.1564), channel_id=1, source_target_pairs={{16,0},{32,16},{48,32},{64,48},{80,64},{96,80},{112,96},{17,1},{33... | collective-permute-start | bytes 1179656 | tf_op jit(solution)/shard_map/while/body/eval_jaxpr/ppermute | solution.py:16
  1040.7 194.8 %collective-permute-start.3 = (bf16[128,1536]{0,1:T(8,128)(2,1)}, bf16[128,1536]{0,1:T(8,128)(2,1)S(1)}, u32[]{:S(2)}, u32[]{:S(2)}) collective-permute-start(bf16[128,1536]{0,1:T(8,128)(2,1)} %get-tuple-element.1565), channel_id=1, source_target_pairs={{0,16},{16,32},{32,48},{48,64},{64,80},{80,96},{96,112},{1,17},{17... | collective-permute-start | bytes 1179656 | tf_op jit(solution)/shard_map/while/body/eval_jaxpr/ppermute | solution.py:16
  1290.5 61.4 %collective-permute-start.2 = (bf16[128,1536]{0,1:T(8,128)(2,1)}, bf16[128,1536]{0,1:T(8,128)(2,1)}, u32[]{:S(2)}, u32[]{:S(2)}) collective-permute-start(bf16[128,1536]{0,1:T(8,128)(2,1)} %get-tuple-element.1564), channel_id=1, source_target_pairs={{16,0},{32,16},{48,32},{64,48},{80,64},{96,80},{112,96},{17,1},{33... | collective-permute-start | bytes 1179656 | tf_op jit(solution)/shard_map/while/body/eval_jaxpr/ppermute | solution.py:16
  1293.3 61.5 %collective-permute-start.3 = (bf16[128,1536]{0,1:T(8,128)(2,1)}, bf16[128,1536]{0,1:T(8,128)(2,1)S(1)}, u32[]{:S(2)}, u32[]{:S(2)}) collective-permute-start(bf16[128,1536]{0,1:T(8,128)(2,1)} %get-tuple-element.1565), channel_id=1, source_target_pairs={{0,16},{16,32},{32,48},{48,64},{64,80},{80,96},{96,112},{1,17},{17... | collective-permute-start | bytes 1179656 | tf_op jit(solution)/shard_map/while/body/eval_jaxpr/ppermute | solution.py:16
  1409.9 11.2 collective-permute-start.2
  1412.6 11.4 collective-permute-start.3
  1447.0 263.9 %reduce-scatter.3.cloned.1.call-start = ((), (), s32[]{:S(2)}) async-start(), calls=%async_computation.3 | async-start | bytes 5013504 | tf_op jit(solution)/shard_map/reduce_scatter | solution.py:199
  1451.6 7.5 copy-start.32
  1451.6 7.5 copy-start.34
  1451.6 7.5 copy-start.36
  1451.6 7.5 copy-start.38
  1483.7 9.0 copy-start.45
  1483.7 9.0 copy-start.49
  1505.8 137.0 %copy-start.64 = (f32[2,128]{1,0:T(2,128)S(1)}, f32[2,128]{1,0:T(2,128)}, u32[]{:S(2)}) copy-start(f32[2,128]{1,0:T(2,128)} %get-tuple-element.741) | copy-start | bytes 3076
  1625.1 7.5 collective-permute-start.10
  1632.6 6.7 collective-permute-start.11
  1639.3 71.6 %collective-permute-start.12 = (bf16[96,1536]{1,0:T(8,128)(2,1)S(1)}, bf16[96,1536]{1,0:T(8,128)(2,1)S(1)}, u32[]{:S(2)}, u32[]{:S(2)}) collective-permute-start(bf16[96,1536]{1,0:T(8,128)(2,1)S(1)} %collective-permute-done.11), channel_id=1, source_target_pairs={{0,64},{16,80},{32,96},{48,112},{64,0},{80,16},{96,32},{112,48},{1... | collective-permute-start | bytes 884744 | tf_op jit(solution)/shard_map/ppermute | solution.py:10
  1676.6 3.6 collective-permute-start.13
  1680.3 3.6 collective-permute-start.14
  1683.8 5.1 collective-permute-start.15
  (92 other events, 353.3 us)
Sparse Core Ops, SparseCore 0:
  10.5 59.5 all-gather.5
  72.5 54.8 all-gather.3
  1447.1 177.8 reduce-scatter.4
  1629.0 81.8 reduce-scatter.2
where the time goes:
time: 1730 us; the launch traced here: 1720 us
  starting transfers between devices  634 us (37%)
  waiting for transfers between devices  341 us (20%)
  local copies, waits for them, and re-layouts  249 us (14%)
  other arithmetic  216 us (12%)
  matrix products  166 us (10%)
  loops' own time  66.5 us (4%)
  blocking collectives  33.8 us (2%)
    ppermute x36, starting transfers between devices, shifted(): return lax.ppermute(block, axis, route)  613 us
    reduce_scatter x1, waiting for transfers between devices, shards(): lax.psum_scatter(sum_far.astype(jnp.bfloat16), 'dp', scatter_dimension=0,...  119 us
    concatenate x22, local copies, waits for them, and re-layouts, rotate(): return jnp.concatenate(pieces, axis=-1)  95.2 us
    ppermute x36, waiting for transfers between devices, shifted(): return lax.ppermute(block, axis, route)  81.8 us
    add x33, other arithmetic, rotate(): pieces.append(lower_half * sine_part + upper_half * cosine)  80 us
    all_gather x1, waiting for transfers between devices, shards(): lax.all_gather(far_weight, 'dp', axis=0, tiled=True)  57.3 us
    dot_general x23, matrix products, mixing(): jnp.einsum('qhe,khe->hqk', queries, key_rows, precision=lax.Precision.HIG...  53.6 us
    dot_general x6, matrix products, phase_backward(): lax.dot_general(mixed_rows, grad_out, (((0,), (0,)), ((), ())), preferred...  52.4 us
  transfers between devices with their start and end apart: 52, of which 37 were waited for; matrix products, arithmetic and copies ran while one was open for 20% of the time, Pallas kernels for 0%

commit v1 on v0

v1 whole, which is shorter than its diff:
```python
import functools
import math

import jax
import jax.numpy as jnp
import numpy as np
from jax import lax
from jax.experimental import pallas as pl
from jax.experimental.pallas import tpu as pltpu
from jax.sharding import PartitionSpec as P

D = 1536
HEAD = 128
TOK = 128
HEADS = D // HEAD
PHASES = 8
F32 = jnp.float32
BF16 = jnp.bfloat16

NN = (((1,), (0,)), ((), ()))
NT = (((1,), (1,)), ((), ()))
TN = (((0,), (0,)), ((), ()))


def dot(a, b, dims=NN, precision=None):
    return lax.dot_general(a, b, dims, precision=precision, preferred_element_type=F32)


def rotary_constants():
    first = HEAD // 8
    rest = (HEAD - first) // 2
    freq = np.zeros((8, HEAD), np.float32)
    partner = np.zeros(HEAD, np.int32)
    sign = np.zeros((1, HEAD), np.float32)
    offset = 0
    for axis, width in enumerate((first, rest, rest)):
        half = width // 2
        values = np.float32(256.0) ** (np.float32(-2.0) * np.arange(half, dtype=np.float32) / np.float32(width))
        low = np.arange(offset, offset + half)
        high = low + half
        freq[axis, low] = values
        freq[axis, high] = values
        partner[low], partner[high] = high, low
        sign[0, low], sign[0, high] = -1.0, 1.0
        offset += width
    swap = np.zeros((HEAD, HEAD), np.float32)
    swap[partner, np.arange(HEAD)] = 1.0
    return freq, swap, sign


def head(j):
    return pl.ds(j * HEAD, HEAD)


def forward_phase(s, w_ref, tabs, swap, hs, qs, ks, es, ms, ns, rcols, icols):
    a0, b0, a1, b1 = tabs
    ones = jnp.ones((TOK, HEAD), BF16)
    for j in range(HEADS):
        hj = hs[s, :, head(j)]
        hf = hj.astype(F32)
        r = lax.rsqrt(jnp.mean(hf * hf, axis=-1, keepdims=True) + 1e-6)
        rcols[s, :, j : j + 1] = r
        n = hf * r
        nsw = dot(hj, swap) * r
        ns[s, :, head(j)] = nsw.astype(BF16)
        qs[s, :, head(j)] = (n * a0 + nsw * b0).astype(BF16)
        ks[s, :, head(j)] = (n * a1 + nsw * b1).astype(BF16)
    for j in range(HEADS):
        scores = dot(qs[s, :, head(j)], ks[s, :, head(j)], NT)
        es[s, :, head(j)] = jnp.exp(scores).astype(BF16)
    for j in range(HEADS):
        both = dot(es[s, :, head(j)], jnp.concatenate([hs[s, :, head(j)], ones], axis=1))
        inv = 1.0 / both[:, HEAD:]
        icols[s, :, j : j + 1] = inv[:, 0:1]
        ms[s, :, head(j)] = (both[:, :HEAD] * inv).astype(BF16)
    for c in range(D // 512):
        cols = pl.ds(c * 512, 512)
        update = dot(ms[s], w_ref[0, :, cols])
        hs[s + 1, :, cols] = (hs[s, :, cols].astype(F32) + update).astype(BF16)


def backward_phase(s, w_ref, tabs, swap, g, gm, acc, hs, qs, ks, es, ms, ns, rcols, icols, grad_ref):
    a0, b0, a1, b1 = tabs
    for c in range(D // 512):
        cols = pl.ds(c * 512, 512)
        gm[:, cols] = dot(g[...], w_ref[0, cols, :], NT).astype(BF16)
    for c in range(D // 512):
        cols = pl.ds(c * 512, 512)
        for t in range(D // 512):
            rows = pl.ds(t * 512, 512)
            grad_ref[0, rows, cols] = dot(ms[s, :, rows], g[:, cols], TN).astype(BF16)
    acc[...] = jnp.zeros_like(acc)
    for j in range(HEADS):
        hj = hs[s, :, head(j)]
        ej = es[s, :, head(j)]
        qj = qs[s, :, head(j)]
        kj = ks[s, :, head(j)]
        r = rcols[s, :, j : j + 1]
        gmf = gm[:, head(j)].astype(F32) * icols[s, :, j : j + 1]
        delta = jnp.sum(gmf * ms[s, :, head(j)].astype(F32), axis=-1, keepdims=True)
        gmb = gmf.astype(BF16)
        ga = dot(gmb, hj, NT)
        ds = (ej.astype(F32) * (ga - delta)).astype(BF16)
        gv = dot(ej, gmb, TN)
        dq = dot(ds, kj)
        dk = dot(ds, qj, TN)
        n = hj.astype(F32) * r
        nsw = ns[s, :, head(j)].astype(F32)
        acc[0] += n * dq
        acc[1] += nsw * dq
        acc[2] += n * dk
        acc[3] += nsw * dk
        crossed = (dq * b0 + dk * b1).astype(BF16)
        dn = dq * a0 + dk * a1 + dot(crossed, swap, NT)
        dh = r * (dn - n * jnp.mean(dn * n, axis=-1, keepdims=True))
        g[:, head(j)] = (g[:, head(j)].astype(F32) + (dh + gv)).astype(BF16)


def compute_kernel(place_ref, clip_ref, pos_ref, cot_ref, gains_ref, swapped_ref, freq_ref, swap_ref, sign_ref, w_ref,
                   grad_ref, dgain_ref, hs, qs, ks, es, ms, ns, rcols, icols, g, gm, acc, cosine, sine):
    step = pl.program_id(0)
    live = place_ref[0] < 6
    scale = 1.0 / math.sqrt(HEAD)
    swap = swap_ref[...]

    def tables(s):
        ga = gains_ref[s].astype(F32)
        gs = swapped_ref[s].astype(F32)
        c, n = cosine[...], sine[...]
        return (c * (ga[0:1] * scale), n * (gs[0:1] * scale), c * ga[1:2], n * gs[1:2])

    saved = (hs, qs, ks, es, ms, ns, rcols, icols)

    @pl.when(live & (step == 0))
    def _():
        p = place_ref[0]
        positions = pos_ref[:, p // 3, p % 3, :].astype(F32)
        padded = jnp.concatenate([positions, jnp.zeros((5, TOK), F32)], axis=0)
        angles = dot(padded, freq_ref[...], TN, lax.Precision.HIGHEST)
        cosine[...] = jnp.cos(angles)
        sine[...] = jnp.sin(angles) * sign_ref[...]
        hs[0] = clip_ref[0, 0]

    @pl.when(live & (step < PHASES))
    def _():
        forward_phase(step, w_ref, tables(step), swap, *saved)

    @pl.when(live & (step == PHASES))
    def _():
        g[...] = cot_ref[0, 0]

    @pl.when(live & (step >= PHASES))
    def _():
        s = 2 * PHASES - 1 - step
        backward_phase(s, w_ref, tables(s), swap, g, gm, acc, *saved, grad_ref)
        x0 = jnp.sum(acc[0] * cosine[...], axis=0, keepdims=True)
        y0 = jnp.sum(acc[1] * sine[...], axis=0, keepdims=True)
        x1 = jnp.sum(acc[2] * cosine[...], axis=0, keepdims=True)
        y1 = jnp.sum(acc[3] * sine[...], axis=0, keepdims=True)
        rows = jnp.concatenate([x0 * scale, x1, y0 * scale, y1, jnp.zeros((4, HEAD), F32)], axis=0)
        dgain_ref[0] = rows

    @pl.when(jnp.logical_not(live) & (step >= PHASES))
    def _():
        grad_ref[...] = jnp.zeros_like(grad_ref)
        dgain_ref[...] = jnp.zeros_like(dgain_ref)


def compute(place, clips, positions, cotangent, gains, swapped, weights):
    freq, swap, sign = rotary_constants()

    def group(i, place_ref):
        p = jnp.minimum(place_ref[0], 5)
        return (p // 3, p % 3)

    def phase_of(i):
        return jnp.minimum(i, 2 * PHASES - 1 - i)

    def out_phase(i):
        return jnp.minimum(2 * PHASES - 1 - i, PHASES - 1)

    whole = lambda rank: (lambda i, p: (0,) * rank)
    spec = pltpu.PrefetchScalarGridSpec(
        num_scalar_prefetch=1,
        grid=(2 * PHASES,),
        in_specs=[
            pl.BlockSpec((1, 1, TOK, D), lambda i, p: (*group(i, p), 0, 0)),
            pl.BlockSpec((3, 2, 3, TOK), whole(4)),
            pl.BlockSpec((1, 1, TOK, D), lambda i, p: (*group(i, p), 0, 0)),
            pl.BlockSpec((PHASES, 2, HEAD), whole(3)),
            pl.BlockSpec((PHASES, 2, HEAD), whole(3)),
            pl.BlockSpec((8, HEAD), whole(2)),
            pl.BlockSpec((HEAD, HEAD), whole(2)),
            pl.BlockSpec((1, HEAD), whole(2)),
            pl.BlockSpec((1, D, D), lambda i, p: (phase_of(i), 0, 0)),
        ],
        out_specs=[
            pl.BlockSpec((1, D, D), lambda i, p: (out_phase(i), 0, 0)),
            pl.BlockSpec((1, 8, HEAD), lambda i, p: (out_phase(i), 0, 0)),
        ],
        scratch_shapes=[
            pltpu.VMEM((PHASES + 1, TOK, D), BF16),
            pltpu.VMEM((PHASES, TOK, D), BF16),
            pltpu.VMEM((PHASES, TOK, D), BF16),
            pltpu.VMEM((PHASES, TOK, D), BF16),
            pltpu.VMEM((PHASES, TOK, D), BF16),
            pltpu.VMEM((PHASES, TOK, D), BF16),
            pltpu.VMEM((PHASES, TOK, HEAD), F32),
            pltpu.VMEM((PHASES, TOK, HEAD), F32),
            pltpu.VMEM((TOK, D), BF16),
            pltpu.VMEM((TOK, D), BF16),
            pltpu.VMEM((4, TOK, HEAD), F32),
            pltpu.VMEM((TOK, HEAD), F32),
            pltpu.VMEM((TOK, HEAD), F32),
        ],
    )
    return pl.pallas_call(
        compute_kernel,
        grid_spec=spec,
        out_shape=(
            jax.ShapeDtypeStruct((PHASES, D, D), BF16),
            jax.ShapeDtypeStruct((PHASES, 8, HEAD), F32),
        ),
        compiler_params=pltpu.CompilerParams(
            dimension_semantics=("arbitrary",), vmem_limit_bytes=60 << 20
        ),
        name="phases",
    )(
        place, clips, positions, cotangent, gains, swapped, jnp.asarray(freq),
        jnp.asarray(swap, BF16), jnp.asarray(sign), weights,
    )


def shards(clips, positions, out_proj, qk_gains, cotangent):
    place = lax.axis_index("pipe")
    _, swap, _ = rotary_constants()
    partner = np.argmax(swap, axis=0)
    weights = lax.all_gather(out_proj[0], ("pipe", "dp"), axis=0, tiled=True).reshape(PHASES, D, D)
    gains = lax.all_gather(qk_gains[0], "pipe", axis=0)
    swapped = gains[:, :, partner]
    grads, dgains = compute(place[None], clips, positions, cotangent, gains, swapped, weights)
    shard = lax.psum_scatter(
        grads.reshape(PHASES * D, D), ("pipe", "dp"), scatter_dimension=0, tiled=True
    )
    total = lax.psum(dgains, ("pipe", "dp"))
    mine = lax.dynamic_index_in_dim(total, place, 0, keepdims=True)
    dgain = mine[:, 0:2] + mine[:, 2:4][:, :, partner]
    return (shard.astype(F32)[None], dgain)


def solution(mesh):
    placed = (
        P(None, None, "dp", None),
        P(None, None, None, "dp"),
        P("pipe", "dp", None),
        P("pipe", None, None),
        P(None, None, "dp", None),
    )
    return jax.shard_map(
        shards,
        mesh=mesh,
        in_specs=placed,
        out_specs=(P("pipe", "dp", None), P("pipe", None, None)),
        check_vma=False,
    )
```

time: 1730 us -> 1030 us (0.60)
  starting transfers between devices: 634 us -> 0.08 us
  waiting for transfers between devices: 341 us -> 856 us
  local copies, waits for them, and re-layouts: 249 us -> 4.41 us
  other arithmetic: 216 us -> 3.08 us
  matrix products: 166 us -> 0 us
  Pallas kernels: 0 us -> 70.2 us
  loops' own time: 66.5 us -> 0 us
  blocking collectives: 33.8 us -> 85.6 us
    ppermute x48 -> x0, starting transfers between devices: 634 us -> none  [the longest x36 613 us: shifted(): return lax.ppermute(block, axis, route)]
    reduce_scatter x2 -> x1, waiting for transfers between devices: 141 us -> 635 us  [shards(): lax.psum_scatter(grads.reshape(PHASES * D, D), ('pipe', 'dp'), scatter_di...]
    dot_general x62 -> x0, matrix products: 166 us -> none  [the longest x23 53.6 us: mixing(): jnp.einsum('qhe,khe->hqk', queries, key_rows, precision=lax.Precision.HIG...]
    all_gather x2 -> x1, waiting for transfers between devices: 74.6 us -> 220 us  [shards(): lax.all_gather(out_proj[0], ('pipe', 'dp'), axis=0, tiled=True)]
    ppermute x48 -> x0, waiting for transfers between devices: 124 us -> none  [the longest x36 81.8 us: shifted(): return lax.ppermute(block, axis, route)]
    concatenate x22 -> x0, local copies, waits for them, and re-layouts: 95.2 us -> none  [rotate(): return jnp.concatenate(pieces, axis=-1)]
    add x39 -> x1, other arithmetic: 83.9 us -> 0.59 us  [shards(): dgain = mine[:, 0:2] + mine[:, 2:4][:, :, partner]]
    pallas_call x0 -> x1, Pallas kernels: none -> 70.2 us  [compute(): pl.pallas_call(compute_kernel, grid_spec=spec, out_shape=(jax.ShapeDtypeS...]
  transfers between devices with their start and end apart: 52 -> 2, of which waited for: 37 -> 2; matrix products, arithmetic and copies ran while one was open for 20% -> 0% of each run, Pallas kernels for 0% -> 0%
where the time goes in v1:
time: 1030 us
  waiting for transfers between devices  856 us (83%)
  blocking collectives  85.6 us (8%)
  Pallas kernels  70.2 us (7%)
  between operations  14.1 us (1%)
    reduce_scatter x1, waiting for transfers between devices, shards(): lax.psum_scatter(grads.reshape(PHASES * D, D), ('pipe', 'dp'), scatter_di...  635 us
    all_gather x1, waiting for transfers between devices, shards(): lax.all_gather(out_proj[0], ('pipe', 'dp'), axis=0, tiled=True)  220 us
    pallas_call x1, Pallas kernels, compute(): pl.pallas_call(compute_kernel, grid_spec=spec, out_shape=(jax.ShapeDtypeS...  70.2 us
    psum x1, blocking collectives, shards(): total = lax.psum(dgains, ('pipe', 'dp'))  66.2 us
  transfers between devices with their start and end apart: 2, of which 2 were waited for; matrix products, arithmetic and copies ran while one was open for 0% of the time, Pallas kernels for 0%

profile of v1, /device:TPU:0, one launch (start us, length us, event | category | flops | bytes accessed | tf_op | source)
XLA Modules:
  0.0 1033.3 jit_solution(14756528502884212722)
XLA Ops:
  7.2 0.0 all-gather.3.cloned.1.call-start
  7.2 0.7 all-gather.3.cloned.1.call-update
  7.9 0.0 reduce-scatter.2.cloned.1.call-start
  7.9 1.3 copy.23.pos_ref
  9.3 19.3 %all_gather.6.gains_ref = bf16[8,2,128]{2,1,0:T(2,128)(2,1)S(1)} all-gather(bf16[1,2,128]{2,1,0:T(2,128)(2,1)} %param.14), channel_id=1, replica_groups=mesh['pipe'=8,'dp'=16] {'pipe'}, dimensions={0}, use_global_device_ids=true | all-gather | bytes 4608 | tf_op jit(solution)/shard_map/all_gather | solution.py:239
  28.6 0.0 copy-start
  28.6 0.1 copy.21
  28.7 0.7 pad_clamp_fusion
  29.4 0.7 gather_fusion
  30.1 0.7 copy.22
  30.8 220.2 %all-gather.3.cloned.1.call-done = bf16[1,12288,1536]{2,1,0:T(8,128)(2,1)} async-done(((bf16[1,96,1536]{2,1,0:T(8,128)(2,1)}), bf16[1,12288,1536]{2,1,0:T(8,128)(2,1)}) %all-gather.3.cloned.1.call-update) | async-done | bytes 37748752 | tf_op jit(solution)/shard_map/all_gather | solution.py:238
  250.9 0.0 copy-done
  251.0 70.2 %phases.1 = (bf16[8,1536,1536]{2,1,0:T(8,128)(2,1)}, f32[8,8,128]{2,1,0:T(8,128)}) custom-call(s32[1]{0:T(128)} %bitcast.place_ref, bf16[2,3,128,1536]{3,2,1,0:T(8,128)(2,1)} %clip_ref.1, s32[3,2,3,128]{3,2,1,0:T(4,128)} %copy.23.pos_ref, bf16[2,3,128,1536]{3,2,1,0:T(8,128)(2,1)} %cot_ref.1, bf16[8,2,128]{2,1,0:T(2,128)(2,1)} %copy-done, ...), custom_call_target="tpu_custom_call" | custom-call | tf_op jit(solution)/shard_map/phases/pallas_call | solution.py:217
  321.2 0.0 copy-start.1
  321.2 0.0 reduce-scatter.2.cloned.1.call-update
  321.2 0.7 copy-done.1
  321.9 66.2 %psum.7 = f32[8,8,128]{2,1,0:T(8,128)S(1)} all-reduce(f32[8,8,128]{2,1,0:T(8,128)S(1)} %copy-done.1), channel_id=1, replica_groups=mesh['pipe'=8,'dp'=16] {'pipe','dp'}, use_global_device_ids=true, to_apply=%region_1.0 | all-reduce | flops 8192 | bytes 65536 | tf_op jit(solution)/shard_map/psum | solution.py:245
  388.2 0.1 copy.24
  388.3 0.6 gather_fusion.1
  389.0 0.1 copy.25
  389.0 0.6 bitcast_add_fusion
  389.6 635.1 %reduce-scatter.2.cloned.1.call-done = bf16[96,1536]{1,0:T(8,128)(2,1)} async-done(((bf16[12288,1536]{1,0:T(8,128)(2,1)}), bf16[96,1536]{1,0:T(8,128)(2,1)}) %reduce-scatter.2.cloned.1.call-update) | async-done | bytes 294928 | tf_op jit(solution)/shard_map/reduce_scatter | solution.py:242
  1024.7 1.8 bitcast_convert_fusion
  (2 shorter events, 0.0 us)
Async XLA Ops:
  7.2 243.8 %all-gather.3.cloned.1.call-start = ((), (), s32[]{:S(2)}) async-start(), calls=%async_computation.2 | async-start | bytes 38043648 | tf_op jit(solution)/shard_map/all_gather | solution.py:238
  7.9 1016.8 %reduce-scatter.2.cloned.1.call-start = ((), (), s32[]{:S(2)}) async-start(), calls=%async_computation.1 | async-start | bytes 38043648 | tf_op jit(solution)/shard_map/reduce_scatter | solution.py:242
  28.6 222.4 %copy-start = (bf16[8,2,128]{2,1,0:T(2,128)(2,1)}, bf16[8,2,128]{2,1,0:T(2,128)(2,1)S(1)}, u32[]{:S(2)}) copy-start(bf16[8,2,128]{2,1,0:T(2,128)(2,1)S(1)} %all_gather.6.gains_ref) | copy-start | bytes 12292
  321.2 0.8 copy-start.1
Sparse Core Ops, SparseCore 0:
  9.7 241.2 all-gather.2
  321.3 703.2 reduce-scatter.1

commit v2 on v1

--- a/solution.py
+++ b/solution.py
@@ -46,6 +46,205 @@
     swap = np.zeros((HEAD, HEAD), np.float32)
     swap[partner, np.arange(HEAD)] = 1.0
     return freq, swap, sign
+
+
+MESH = pl.DeviceIdType.MESH
+AXES = "xyz"
+ORDERS = ("xyz", "yzx", "zxy")
+
+
+class Place:
+    def __init__(self):
+        self.pipe = lax.axis_index("pipe")
+        self.dp = lax.axis_index("dp")
+        self.core = self.dp % 2
+        self.at = {
+            "x": self.dp // 8 * 2 + self.pipe % 2,
+            "y": self.pipe // 2,
+            "z": self.dp // 2 % 4,
+        }
+
+    def device(self, core=None, **moved):
+        c = {**self.at, **moved}
+        core = self.core if core is None else core
+        return (c["y"] * 2 + c["x"] % 2, (c["x"] // 2 * 4 + c["z"]) * 2 + core)
+
+    def step(self, axis, delta):
+        return (self.at[axis] + delta + 4) % 4
+
+    def neighbour(self, axis, delta):
+        return self.device(**{axis: self.step(axis, delta)})
+
+    def sibling(self):
+        return self.device(core=1 - self.core)
+
+
+def greet(place):
+    barrier = pltpu.get_barrier_semaphore()
+    others = [place.neighbour(axis, delta) for axis in AXES for delta in (1, -1, 2)]
+    others.append(place.sibling())
+    others += [((place.pipe + q) % PHASES, place.dp) for q in range(1, PHASES)]
+    for other in others:
+        pl.semaphore_signal(barrier, inc=1, device_id=other, device_id_type=MESH)
+    pl.semaphore_wait(barrier, len(others))
+
+
+WHOLE = "whole"
+
+
+def half(h):
+    return ("half", h)
+
+
+def block(ref, lead, k, core, x, y, z):
+    def plain(v):
+        if v is WHOLE:
+            return slice(None)
+        return pl.ds(2 * v[1], 2) if isinstance(v, tuple) else v
+
+    if x is WHOLE:
+        xh, xl = slice(None), slice(None)
+    elif isinstance(x, tuple):
+        xh, xl = x[1], slice(None)
+    else:
+        xh, xl = x // 2, x % 2
+    return ref.at[(*lead, plain(y), xh, plain(z), core, xl, k)]
+
+
+TILES = (4, 2, 4, 2, 2, 3, 16, D // 4)
+
+
+def gather_kernel(shard_ref, gain_ref, w_ref, gains_ref, first_send, first_recv, gain_send, gain_recv, local_sem, send, recv):
+    place = Place()
+    greet(place)
+    me = place.pipe
+    mine = dict(place.at)
+
+    def first(q, owner, target):
+        return pltpu.make_async_remote_copy(
+            src_ref=shard_ref.at[0, q % 2, :, :, pl.ds(pl.multiple_of(q // 2 * (D // 4), 128), D // 4)],
+            dst_ref=w_ref.at[owner, q // 2, place.dp // 8, place.dp // 2 % 4, place.core, q % 2],
+            send_sem=first_send.at[q],
+            recv_sem=first_recv.at[owner],
+            device_id=(target, place.dp),
+            device_id_type=MESH,
+        )
+
+    def gain(owner, q):
+        return pltpu.make_async_remote_copy(
+            src_ref=gain_ref.at[0],
+            dst_ref=gains_ref.at[owner],
+            send_sem=gain_send.at[q],
+            recv_sem=gain_recv.at[owner],
+            device_id=(q, place.dp),
+            device_id_type=MESH,
+        )
+
+    own = pltpu.make_async_copy(
+        shard_ref.at[0, me % 2, :, :, pl.ds(pl.multiple_of(me // 2 * (D // 4), 128), D // 4)],
+        w_ref.at[me, me // 2, place.dp // 8, place.dp // 2 % 4, place.core, me % 2],
+        local_sem.at[0],
+    )
+    own_gain = pltpu.make_async_copy(gain_ref.at[0], gains_ref.at[me], local_sem.at[1])
+    own.start()
+    own_gain.start()
+    for q in range(PHASES):
+        @pl.when(q != me)
+        def _():
+            first(q, me, q).start()
+            gain(me, q).start()
+    for q in range(PHASES):
+        @pl.when(q != me)
+        def _():
+            first(q, me, q).wait_send()
+            gain(me, q).wait_send()
+            first(q, q, q).wait_recv()
+            gain(q, q).wait_recv()
+    own.wait()
+    own_gain.wait()
+
+    def copies(stage, s, parity):
+        made = []
+
+        def add(view, device):
+            i = stage_base[stage] + len(made)
+            made.append(pltpu.make_async_remote_copy(
+                src_ref=view,
+                dst_ref=view,
+                send_sem=send.at[parity, i],
+                recv_sem=recv.at[parity, i],
+                device_id=device,
+                device_id_type=MESH,
+            ))
+
+        if stage == 5:
+            add(w_ref.at[s, :, :, :, place.core], place.sibling())
+            return made
+        for k, (a, b, c) in enumerate(ORDERS):
+            def view(**where):
+                return block(w_ref, (s,), k, place.core, **{**mine, **where})
+
+            if stage == 0:
+                for delta in (1, -1, 2):
+                    add(view(), place.neighbour(c, delta))
+            elif stage == 1:
+                for delta in (1, -1):
+                    add(view(**{c: WHOLE}), place.neighbour(b, delta))
+            elif stage == 2:
+                for h, delta in enumerate((1, -1)):
+                    add(view(**{b: place.step(b, -delta), c: half(h)}), place.neighbour(b, delta))
+            elif stage == 3:
+                for delta in (1, -1):
+                    add(view(**{b: WHOLE, c: WHOLE}), place.neighbour(a, delta))
+            else:
+                for h, delta in enumerate((1, -1)):
+                    add(view(**{a: place.step(a, -delta), b: half(h), c: WHOLE}), place.neighbour(a, delta))
+        return made
+
+    stage_base = (0, 9, 15, 21, 27, 33)
+
+    def tick(t, carry):
+        for stage in range(6):
+            s = t - 1 - stage
+
+            @pl.when((s >= 0) & (s < PHASES))
+            def _():
+                for copy in copies(stage, s, (t + 1) % 2):
+                    copy.wait()
+        for stage in range(6):
+            s = t - stage
+
+            @pl.when((s >= 0) & (s < PHASES))
+            def _():
+                for copy in copies(stage, s, t % 2):
+                    copy.start()
+        return carry
+
+    lax.fori_loop(0, PHASES + 6, tick, 0)
+
+
+def gather(shard, gain_rows):
+    anywhere = pl.BlockSpec(memory_space=pl.ANY)
+    return pl.pallas_call(
+        gather_kernel,
+        out_shape=(
+            jax.ShapeDtypeStruct((PHASES, *TILES), BF16),
+            jax.ShapeDtypeStruct((PHASES, 8, HEAD), F32),
+        ),
+        in_specs=[anywhere, anywhere],
+        out_specs=[anywhere, anywhere],
+        scratch_shapes=[
+            pltpu.SemaphoreType.DMA((PHASES,)),
+            pltpu.SemaphoreType.DMA((PHASES,)),
+            pltpu.SemaphoreType.DMA((PHASES,)),
+            pltpu.SemaphoreType.DMA((PHASES,)),
+            pltpu.SemaphoreType.DMA((2,)),
+            pltpu.SemaphoreType.DMA((2, 34)),
+            pltpu.SemaphoreType.DMA((2, 34)),
+        ],
+        compiler_params=pltpu.CompilerParams(collective_id=0, has_side_effects=True),
+        name="gather",
+    )(shard, gain_rows)
 
 
 def head(j):
@@ -73,9 +272,9 @@
         inv = 1.0 / both[:, HEAD:]
         icols[s, :, j : j + 1] = inv[:, 0:1]
         ms[s, :, head(j)] = (both[:, :HEAD] * inv).astype(BF16)
-    for c in range(D // 512):
-        cols = pl.ds(c * 512, 512)
-        update = dot(ms[s], w_ref[0, :, cols])
+    for c in range(4):
+        cols = pl.ds(c * 384, 384)
+        update = dot(ms[s], w_ref[0, c])
         hs[s + 1, :, cols] = (hs[s, :, cols].astype(F32) + update).astype(BF16)
 
 
@@ -83,7 +282,10 @@
     a0, b0, a1, b1 = tabs
     for c in range(D // 512):
         cols = pl.ds(c * 512, 512)
-        gm[:, cols] = dot(g[...], w_ref[0, cols, :], NT).astype(BF16)
+        total = dot(g[:, 0:384], w_ref[0, 0, cols, :], NT)
+        for y in range(1, 4):
+            total += dot(g[:, pl.ds(y * 384, 384)], w_ref[0, y, cols, :], NT)
+        gm[:, cols] = total.astype(BF16)
     for c in range(D // 512):
         cols = pl.ds(c * 512, 512)
         for t in range(D // 512):
@@ -116,7 +318,7 @@
         g[:, head(j)] = (g[:, head(j)].astype(F32) + (dh + gv)).astype(BF16)
 
 
-def compute_kernel(place_ref, clip_ref, pos_ref, cot_ref, gains_ref, swapped_ref, freq_ref, swap_ref, sign_ref, w_ref,
+def compute_kernel(place_ref, clip_ref, pos_ref, cot_ref, gains_ref, freq_ref, swap_ref, sign_ref, w_ref,
                    grad_ref, dgain_ref, hs, qs, ks, es, ms, ns, rcols, icols, g, gm, acc, cosine, sine):
     step = pl.program_id(0)
     live = place_ref[0] < 6
@@ -124,10 +326,9 @@
     swap = swap_ref[...]
 
     def tables(s):
-        ga = gains_ref[s].astype(F32)
-        gs = swapped_ref[s].astype(F32)
+        rows = gains_ref[s]
         c, n = cosine[...], sine[...]
-        return (c * (ga[0:1] * scale), n * (gs[0:1] * scale), c * ga[1:2], n * gs[1:2])
+        return (c * (rows[0:1] * scale), n * (rows[2:3] * scale), c * rows[1:2], n * rows[3:4])
 
     saved = (hs, qs, ks, es, ms, ns, rcols, icols)
 
@@ -166,7 +367,7 @@
         dgain_ref[...] = jnp.zeros_like(dgain_ref)
 
 
-def compute(place, clips, positions, cotangent, gains, swapped, weights):
+def compute(place, clips, positions, cotangent, gains, weights):
     freq, swap, sign = rotary_constants()
 
     def group(i, place_ref):
@@ -187,12 +388,11 @@
             pl.BlockSpec((1, 1, TOK, D), lambda i, p: (*group(i, p), 0, 0)),
             pl.BlockSpec((3, 2, 3, TOK), whole(4)),
             pl.BlockSpec((1, 1, TOK, D), lambda i, p: (*group(i, p), 0, 0)),
-            pl.BlockSpec((PHASES, 2, HEAD), whole(3)),
-            pl.BlockSpec((PHASES, 2, HEAD), whole(3)),
+            pl.BlockSpec((PHASES, 8, HEAD), whole(3)),
             pl.BlockSpec((8, HEAD), whole(2)),
             pl.BlockSpec((HEAD, HEAD), whole(2)),
             pl.BlockSpec((1, HEAD), whole(2)),
-            pl.BlockSpec((1, D, D), lambda i, p: (phase_of(i), 0, 0)),
+            pl.BlockSpec((1, 4, D, D // 4), lambda i, p: (phase_of(i), 0, 0, 0)),
         ],
         out_specs=[
             pl.BlockSpec((1, D, D), lambda i, p: (out_phase(i), 0, 0)),
@@ -226,7 +426,7 @@
         ),
         name="phases",
     )(
-        place, clips, positions, cotangent, gains, swapped, jnp.asarray(freq),
+        place, clips, positions, cotangent, gains, jnp.asarray(freq),
         jnp.asarray(swap, BF16), jnp.asarray(sign), weights,
     )
 
@@ -235,10 +435,11 @@
     place = lax.axis_index("pipe")
     _, swap, _ = rotary_constants()
     partner = np.argmax(swap, axis=0)
-    weights = lax.all_gather(out_proj[0], ("pipe", "dp"), axis=0, tiled=True).reshape(PHASES, D, D)
-    gains = lax.all_gather(qk_gains[0], "pipe", axis=0)
-    swapped = gains[:, :, partner]
-    grads, dgains = compute(place[None], clips, positions, cotangent, gains, swapped, weights)
+    own = qk_gains[0].astype(F32)
+    gain_rows = jnp.concatenate([own, own[:, partner], jnp.zeros((4, HEAD), F32)], axis=0)[None]
+    tiles, gains = gather(out_proj.reshape(1, 2, 3, 16, D), gain_rows)
+    weights = tiles.reshape(PHASES, 4, D, D // 4)
+    grads, dgains = compute(place[None], clips, positions, cotangent, gains, weights)
     shard = lax.psum_scatter(
         grads.reshape(PHASES * D, D), ("pipe", "dp"), scatter_dimension=0, tiled=True
     )

time: 1030 us -> 903 us (0.88)
  waiting for transfers between devices: 856 us -> 636 us
  Pallas kernels: 70.2 us -> 179 us
  blocking collectives: 85.6 us -> 65.9 us
    all_gather x1 -> x0, waiting for transfers between devices: 220 us -> none  [shards(): lax.all_gather(out_proj[0], ('pipe', 'dp'), axis=0, tiled=True)]
    pallas_call x0 -> x1, Pallas kernels: none -> 109 us  [gather(): pl.pallas_call(gather_kernel, out_shape=(jax.ShapeDtypeStruct((PHASES, *T...]
    all_gather x1 -> x0, blocking collectives: 19.3 us -> none  [shards(): gains = lax.all_gather(qk_gains[0], 'pipe', axis=0)]
  transfers between devices with their start and end apart: 2 -> 1, of which waited for: 2 -> 1; matrix products, arithmetic and copies ran while one was open for 0% -> 0% of each run, Pallas kernels for 0% -> 0%
where the time goes in v2:
time: 903 us
  waiting for transfers between devices  636 us (70%)
  Pallas kernels  179 us (20%)
  blocking collectives  65.9 us (7%)
  between operations  14 us (2%)
    reduce_scatter x1, waiting for transfers between devices, shards(): lax.psum_scatter(grads.reshape(PHASES * D, D), ('pipe', 'dp'), scatter_di...  636 us
    pallas_call x1, Pallas kernels, gather(): pl.pallas_call(gather_kernel, out_shape=(jax.ShapeDtypeStruct((PHASES, *T...  109 us
    pallas_call x1, Pallas kernels, compute(): pl.pallas_call(compute_kernel, grid_spec=spec, out_shape=(jax.ShapeDtypeS...  70.5 us
    psum x1, blocking collectives, shards(): total = lax.psum(dgains, ('pipe', 'dp'))  65.9 us
  transfers between devices with their start and end apart: 1, of which 1 were waited for; matrix products, arithmetic and copies ran while one was open for 0% of the time, Pallas kernels for 0%

profile of v2, /device:TPU:0, one launch (start us, length us, event | category | flops | bytes accessed | tf_op | source)
XLA Modules:
  0.0 902.9 jit_solution(9485274775138743865)
XLA Ops:
  7.2 0.0 reduce-scatter.2.cloned.1.call-start
  7.2 0.7 bitcast_convert_fusion.1
  7.9 0.1 copy.13
  8.0 0.7 pad_clamp_fusion
  8.6 0.6 gather_fusion
  9.3 0.1 copy.14
  9.3 1.3 copy.15.pos_ref
  10.7 0.1 pad.2.clone
  10.8 0.7 maximum_bitcast_fusion.gain_ref
  11.4 108.6 %gather.14 = (bf16[8,4,2,4,2,2,3,16,384]{8,7,6,5,4,3,2,1,0:T(8,128)(2,1)}, f32[8,8,128]{2,1,0:T(8,128)}) custom-call(bf16[1,2,3,16,1536]{4,3,2,1,0:T(8,128)(2,1)} %bitcast.21, f32[1,8,128]{2,1,0:T(8,128)} %maximum_bitcast_fusion.gain_ref), custom_call_target="tpu_custom_call" | custom-call | tf_op jit(solution)/shard_map/gather/pallas_call | solution.py:228
  120.1 70.5 %phases.1 = (bf16[8,1536,1536]{2,1,0:T(8,128)(2,1)}, f32[8,8,128]{2,1,0:T(8,128)}) custom-call(s32[1]{0:T(128)} %bitcast.place_ref, bf16[2,3,128,1536]{3,2,1,0:T(8,128)(2,1)} %clip_ref.1, s32[3,2,3,128]{3,2,1,0:T(4,128)} %copy.15.pos_ref, bf16[2,3,128,1536]{3,2,1,0:T(8,128)(2,1)} %cot_ref.1, f32[8,8,128]{2,1,0:T(8,128)} %get-tuple-element.6.gains_ref, ...), custom_call_target="tpu_custom_call" | custom-call | tf_op jit(solution)/shard_map/phases/pallas_call | solution.py:417
  190.5 0.0 copy-start
  190.6 0.0 reduce-scatter.2.cloned.1.call-update
  190.6 0.7 copy-done
  191.3 65.9 %psum.7 = f32[8,8,128]{2,1,0:T(8,128)S(1)} all-reduce(f32[8,8,128]{2,1,0:T(8,128)S(1)} %copy-done), channel_id=1, replica_groups=mesh['pipe'=8,'dp'=16] {'pipe','dp'}, use_global_device_ids=true, to_apply=%region_1.0 | all-reduce | flops 8192 | bytes 65536 | tf_op jit(solution)/shard_map/psum | solution.py:446
  257.2 0.1 copy.16
  257.3 0.6 gather_fusion.1
  258.0 0.1 copy.17
  258.0 0.6 bitcast_add_fusion
  258.6 635.6 %reduce-scatter.2.cloned.1.call-done = bf16[96,1536]{1,0:T(8,128)(2,1)} async-done(((bf16[12288,1536]{1,0:T(8,128)(2,1)}), bf16[96,1536]{1,0:T(8,128)(2,1)}) %reduce-scatter.2.cloned.1.call-update) | async-done | bytes 294928 | tf_op jit(solution)/shard_map/reduce_scatter | solution.py:443
  894.3 1.8 bitcast_convert_fusion
  (3 shorter events, 0.0 us)
Async XLA Ops:
  7.2 887.1 %reduce-scatter.2.cloned.1.call-start = ((), (), s32[]{:S(2)}) async-start(), calls=%async_computation.1 | async-start | bytes 38043648 | tf_op jit(solution)/shard_map/reduce_scatter | solution.py:443
  190.5 0.8 copy-start
Sparse Core Ops, SparseCore 0:
  190.7 703.5 reduce-scatter.1

commit v3 on v2

--- a/solution.py
+++ b/solution.py
@@ -79,11 +79,13 @@
         return self.device(core=1 - self.core)
 
 
-def greet(place):
+def greet(place, wide=False):
     barrier = pltpu.get_barrier_semaphore()
     others = [place.neighbour(axis, delta) for axis in AXES for delta in (1, -1, 2)]
     others.append(place.sibling())
     others += [((place.pipe + q) % PHASES, place.dp) for q in range(1, PHASES)]
+    if wide:
+        others += [(place.pipe, (place.dp + q) % WIDE_PEERS) for q in range(1, WIDE_PEERS)]
     for other in others:
         pl.semaphore_signal(barrier, inc=1, device_id=other, device_id_type=MESH)
     pl.semaphore_wait(barrier, len(others))
@@ -245,6 +247,276 @@
         compiler_params=pltpu.CompilerParams(collective_id=0, has_side_effects=True),
         name="gather",
     )(shard, gain_rows)
+
+
+STRIP = (3, 16, D // 4)
+STAGE_BASE = (0, 1, 7, 13, 19, 25)
+WIDE_PEERS = 16
+
+
+def cut(ref, lead, k, where):
+    index = []
+    for axis in ORDERS[k]:
+        if axis in where:
+            v = where[axis]
+            index.append(pl.ds(2 * v[1], 2) if isinstance(v, tuple) else v)
+    return ref.at[(*lead, *index)]
+
+
+def add_into(out, *parts):
+    total = parts[0][...].astype(F32)
+    for part in parts[1:]:
+        total += part[...].astype(F32)
+    out[...] = total.astype(out.dtype)
+
+
+class Scatter:
+    def __init__(self, place, bufs):
+        self.place = place
+        (self.grad, self.pair, self.wide, self.wide_half, self.wide_got, self.slim, self.slim_half,
+         self.slim_got, self.last, self.last_got, self.final, self.out, self.send, self.recv,
+         self.final_send, self.final_recv) = bufs
+
+    def copies(self, stage, i):
+        place, slot = self.place, i % 2
+        made = []
+
+        def add(src, dst, device):
+            j = STAGE_BASE[stage] + len(made)
+            made.append(pltpu.make_async_remote_copy(
+                src_ref=src, dst_ref=dst, send_sem=self.send.at[slot, j], recv_sem=self.recv.at[slot, j],
+                device_id=device, device_id_type=MESH))
+
+        if stage == 0:
+            add(self.grad.at[slot, :, :, :, 1 - place.core], self.pair.at[slot], place.sibling())
+            return made
+        for k, (a, b, c) in enumerate(ORDERS):
+            if stage == 1:
+                for h, delta in enumerate((1, -1)):
+                    src = cut(self.wide, (slot, k), k, {a: place.step(a, 2), b: half(h)})
+                    add(src, self.wide_half.at[slot, k, h], place.neighbour(a, delta))
+            elif stage == 2:
+                for h, delta in enumerate((1, -1)):
+                    src = cut(self.wide, (slot, k), k, {a: place.step(a, delta)})
+                    add(src, self.wide_got.at[slot, k, h], place.neighbour(a, delta))
+            elif stage == 3:
+                for h, delta in enumerate((1, -1)):
+                    src = self.slim.at[slot, k, place.step(b, 2), pl.ds(2 * h, 2)]
+                    add(src, self.slim_half.at[slot, k, h], place.neighbour(b, delta))
+            elif stage == 4:
+                for h, delta in enumerate((1, -1)):
+                    src = self.slim.at[slot, k, place.step(b, delta)]
+                    add(src, self.slim_got.at[slot, k, h], place.neighbour(b, delta))
+            else:
+                for h, delta in enumerate((1, -1, 2)):
+                    src = self.last.at[slot, k, place.step(c, delta)]
+                    add(src, self.last_got.at[slot, k, h], place.neighbour(c, delta))
+        return made
+
+    def fill_wide(self, i):
+        slot = i % 2
+        core = self.place.core
+
+        def row(y, carry):
+            for xh in range(2):
+                for xl in range(2):
+                    x = xh * 2 + xl
+                    for k in range(3):
+                        full = slice(None)
+                        where = {"x": x, "y": y, "z": full}
+                        out = self.wide.at[(slot, k, *(where[axis] for axis in ORDERS[k]))]
+                        add_into(out, self.grad.at[slot, y, xh, :, core, xl, k], self.pair.at[slot, y, xh, :, xl, k])
+            return carry
+
+        lax.fori_loop(0, 4, row, 0)
+
+    def process(self, stage, i):
+        place, slot = self.place, i % 2
+        if stage == 1:
+            self.fill_wide(i)
+            return
+        for k, (a, b, c) in enumerate(ORDERS):
+            if stage == 2:
+                for h, delta in enumerate((1, -1)):
+                    part = self.wide.at[slot, k, place.step(a, delta), pl.ds(2 * h, 2)]
+                    add_into(part, part, self.wide_half.at[slot, k, h])
+            elif stage == 3:
+                add_into(self.slim.at[slot, k], self.wide.at[slot, k, place.at[a]],
+                         self.wide_got.at[slot, k, 0], self.wide_got.at[slot, k, 1])
+            elif stage == 4:
+                for h, delta in enumerate((1, -1)):
+                    part = self.slim.at[slot, k, place.step(b, delta), pl.ds(2 * h, 2)]
+                    add_into(part, part, self.slim_half.at[slot, k, h])
+            elif stage == 5:
+                add_into(self.last.at[slot, k], self.slim.at[slot, k, place.at[b]],
+                         self.slim_got.at[slot, k, 0], self.slim_got.at[slot, k, 1])
+            else:
+                add_into(self.final.at[PHASES - 1 - i, k], self.last.at[slot, k, place.at[c]],
+                         *(self.last_got.at[slot, k, h] for h in range(3)))
+
+    def final_copy(self, s, source, target):
+        return pltpu.make_async_remote_copy(
+            src_ref=self.final.at[s], dst_ref=self.out.at[source],
+            send_sem=self.final_send.at[s], recv_sem=self.final_recv.at[source],
+            device_id=(target, self.place.dp), device_id_type=MESH)
+
+    def deliver(self, i):
+        me, s = self.place.pipe, PHASES - 1 - i
+
+        @pl.when(s != me)
+        def _():
+            self.final_copy(s, me, s).start()
+
+        @pl.when(s == me)
+        def _():
+            self.out[s] = self.final[s]
+
+    def settle(self):
+        for q in range(PHASES):
+            @pl.when(q != self.place.pipe)
+            def _():
+                self.final_copy(q, q, q).wait()
+
+    def tick(self, t, first):
+        def each(body, order, lag):
+            for stage in order:
+                i = t - first - stage - lag
+
+                @pl.when((i >= 0) & (i < PHASES))
+                def _():
+                    body(stage, i)
+
+        def wait(stage, i):
+            for copy in self.copies(stage, i):
+                copy.wait()
+
+        def start(stage, i):
+            if stage == 6:
+                self.deliver(i)
+                return
+            for copy in self.copies(stage, i):
+                copy.start()
+
+        each(wait, range(6), 1)
+        each(self.process, (6, 5, 4, 3, 2, 1), 0)
+        each(start, range(7), 0)
+
+
+def scatter_kernel(grads_ref, dgain_ref, out_ref, total_ref, grad, *rest):
+    *bufs, gain_rows, gain_wide, gain_sum, gain_send, gain_recv, wide_send, wide_recv, local_sem = rest
+    place = Place()
+    greet(place, wide=True)
+    scatter = Scatter(place, (grad, *bufs))
+    me = place.pipe
+
+    def gain(owner, source, target):
+        return pltpu.make_async_remote_copy(
+            src_ref=dgain_ref.at[owner], dst_ref=gain_rows.at[source],
+            send_sem=gain_send.at[owner], recv_sem=gain_recv.at[source],
+            device_id=(target, place.dp), device_id_type=MESH)
+
+    def gain_share(index, source, target):
+        return pltpu.make_async_remote_copy(
+            src_ref=gain_sum, dst_ref=gain_wide.at[source],
+            send_sem=wide_send.at[index], recv_sem=wide_recv.at[source],
+            device_id=(me, target), device_id_type=MESH)
+
+    for q in range(PHASES):
+        @pl.when(q != me)
+        def _():
+            gain(q, me, q).start()
+
+        @pl.when(q == me)
+        def _():
+            gain_rows[q] = dgain_ref[q]
+    for q in range(PHASES):
+        @pl.when(q != me)
+        def _():
+            gain(q, q, q).wait()
+    gain_sum[...] = jnp.sum(gain_rows[...], axis=0)
+    for q in range(WIDE_PEERS):
+        @pl.when(q != place.dp)
+        def _():
+            gain_share(q, place.dp, q).start()
+
+        @pl.when(q == place.dp)
+        def _():
+            gain_wide[q] = gain_sum[...]
+
+    def load(i):
+        return pltpu.make_async_copy(grads_ref.at[PHASES - 1 - i], grad.at[i % 2], local_sem.at[i % 2])
+
+    def tick(t, carry):
+        @pl.when((t >= 1) & (t <= PHASES))
+        def _():
+            load(t - 1).wait()
+
+        scatter.tick(t, 1)
+
+        @pl.when(t < PHASES)
+        def _():
+            load(t).start()
+
+        return carry
+
+    lax.fori_loop(0, PHASES + 7, tick, 0)
+    for q in range(WIDE_PEERS):
+        @pl.when(q != place.dp)
+        def _():
+            gain_share(q, q, q).wait()
+    total_ref[...] = jnp.sum(gain_wide[...], axis=0)
+    scatter.settle()
+    for y in range(4):
+        for xl in range(2):
+            out_ref[xl, :, :, pl.ds(y * (D // 4), D // 4)] = scatter.out[y * 2 + xl].astype(F32)
+
+
+def scatter_scratch():
+    piece = (16, D // 4)
+    sems = pltpu.SemaphoreType.DMA
+    return [
+        pltpu.VMEM((2, *TILES), BF16),
+        pltpu.VMEM((2, 4, 2, 4, 2, *STRIP), BF16),
+        pltpu.VMEM((2, 3, 4, 4, 4, *piece), BF16),
+        pltpu.VMEM((2, 3, 2, 2, 4, *piece), BF16),
+        pltpu.VMEM((2, 3, 2, 4, 4, *piece), BF16),
+        pltpu.VMEM((2, 3, 4, 4, *piece), BF16),
+        pltpu.VMEM((2, 3, 2, 2, *piece), BF16),
+        pltpu.VMEM((2, 3, 2, 4, *piece), BF16),
+        pltpu.VMEM((2, 3, 4, *piece), BF16),
+        pltpu.VMEM((2, 3, 3, *piece), BF16),
+        pltpu.VMEM((PHASES, *STRIP), BF16),
+        pltpu.VMEM((PHASES, *STRIP), BF16),
+        sems((2, 34)),
+        sems((2, 34)),
+        sems((PHASES,)),
+        sems((PHASES,)),
+        pltpu.VMEM((PHASES, 8, HEAD), F32),
+        pltpu.VMEM((WIDE_PEERS, 8, HEAD), F32),
+        pltpu.VMEM((8, HEAD), F32),
+        sems((PHASES,)),
+        sems((PHASES,)),
+        sems((WIDE_PEERS,)),
+        sems((WIDE_PEERS,)),
+        sems((2,)),
+    ]
+
+
+def scatter(grads, dgains):
+    return pl.pallas_call(
+        scatter_kernel,
+        out_shape=(
+            jax.ShapeDtypeStruct((2, 3, 16, D), F32),
+            jax.ShapeDtypeStruct((8, HEAD), F32),
+        ),
+        in_specs=[pl.BlockSpec(memory_space=pl.ANY), pl.BlockSpec(memory_space=pltpu.VMEM)],
+        out_specs=[pl.BlockSpec(memory_space=pltpu.VMEM)] * 2,
+        scratch_shapes=scatter_scratch(),
+        compiler_params=pltpu.CompilerParams(
+            collective_id=1, has_side_effects=True, vmem_limit_bytes=60 << 20
+        ),
+        name="scatter",
+    )(grads, dgains)
 
 
 def head(j):
@@ -286,11 +558,11 @@
         for y in range(1, 4):
             total += dot(g[:, pl.ds(y * 384, 384)], w_ref[0, y, cols, :], NT)
         gm[:, cols] = total.astype(BF16)
-    for c in range(D // 512):
-        cols = pl.ds(c * 512, 512)
+    for y in range(4):
+        cols = pl.ds(y * 384, 384)
         for t in range(D // 512):
             rows = pl.ds(t * 512, 512)
-            grad_ref[0, rows, cols] = dot(ms[s, :, rows], g[:, cols], TN).astype(BF16)
+            grad_ref[0, y, rows] = dot(ms[s, :, rows], g[:, cols], TN).astype(BF16)
     acc[...] = jnp.zeros_like(acc)
     for j in range(HEADS):
         hj = hs[s, :, head(j)]
@@ -395,7 +667,7 @@
             pl.BlockSpec((1, 4, D, D // 4), lambda i, p: (phase_of(i), 0, 0, 0)),
         ],
         out_specs=[
-            pl.BlockSpec((1, D, D), lambda i, p: (out_phase(i), 0, 0)),
+            pl.BlockSpec((1, 4, D, D // 4), lambda i, p: (out_phase(i), 0, 0, 0)),
             pl.BlockSpec((1, 8, HEAD), lambda i, p: (out_phase(i), 0, 0)),
         ],
         scratch_shapes=[
@@ -418,7 +690,7 @@
         compute_kernel,
         grid_spec=spec,
         out_shape=(
-            jax.ShapeDtypeStruct((PHASES, D, D), BF16),
+            jax.ShapeDtypeStruct((PHASES, 4, D, D // 4), BF16),
             jax.ShapeDtypeStruct((PHASES, 8, HEAD), F32),
         ),
         compiler_params=pltpu.CompilerParams(
@@ -440,13 +712,9 @@
     tiles, gains = gather(out_proj.reshape(1, 2, 3, 16, D), gain_rows)
     weights = tiles.reshape(PHASES, 4, D, D // 4)
     grads, dgains = compute(place[None], clips, positions, cotangent, gains, weights)
-    shard = lax.psum_scatter(
-        grads.reshape(PHASES * D, D), ("pipe", "dp"), scatter_dimension=0, tiled=True
-    )
-    total = lax.psum(dgains, ("pipe", "dp"))
-    mine = lax.dynamic_index_in_dim(total, place, 0, keepdims=True)
-    dgain = mine[:, 0:2] + mine[:, 2:4][:, :, partner]
-    return (shard.astype(F32)[None], dgain)
+    shard, total = scatter(grads.reshape(PHASES, *TILES), dgains)
+    dgain = total[0:2] + total[2:4][:, partner]
+    return (shard.reshape(1, D // 16, D), dgain[None])
 
 
 def solution(mesh):

time: 903 us -> 313 us (0.35)
  waiting for transfers between devices: 636 us -> 0 us
  Pallas kernels: 179 us -> 302 us
  blocking collectives: 65.9 us -> 0 us
  between operations: 14 us -> 0.66 us
    reduce_scatter x1 -> x0, waiting for transfers between devices: 636 us -> none  [shards(): lax.psum_scatter(grads.reshape(PHASES * D, D), ('pipe', 'dp'), scatter_di...]
    pallas_call x0 -> x1, Pallas kernels: none -> 123 us  [scatter(): pl.pallas_call(scatter_kernel, out_shape=(jax.ShapeDtypeStruct((2, 3, 16,...]
    psum x1 -> x0, blocking collectives: 65.9 us -> none  [shards(): total = lax.psum(dgains, ('pipe', 'dp'))]
  transfers between devices with their start and end apart: 1 -> 0, of which waited for: 1 -> 0; matrix products, arithmetic and copies ran while one was open for 0% -> 0% of each run, Pallas kernels for 0% -> 0%
where the time goes in v3:
time: 313 us; the launch traced here: 312 us
  Pallas kernels  302 us (96%)
  local copies, waits for them, and re-layouts  5.6 us (2%)
  other arithmetic  3.27 us (1%)
    pallas_call x1, Pallas kernels, scatter(): pl.pallas_call(scatter_kernel, out_shape=(jax.ShapeDtypeStruct((2, 3, 16,...  123 us
    pallas_call x1, Pallas kernels, gather(): pl.pallas_call(gather_kernel, out_shape=(jax.ShapeDtypeStruct((PHASES, *T...  109 us
    pallas_call x1, Pallas kernels, compute(): pl.pallas_call(compute_kernel, grid_spec=spec, out_shape=(jax.ShapeDtypeS...  70.6 us

profile of v3, /device:TPU:0, one launch (start us, length us, event | category | flops | bytes accessed | tf_op | source)
XLA Modules:
  0.0 311.9 jit_solution(6553081010234484788)
XLA Ops:
  0.6 0.1 pad.2.clone
  0.7 0.7 bitcast_convert_fusion
  1.4 0.7 pad_clamp_fusion
  2.0 1.3 copy.15.pos_ref
  3.3 0.1 copy.13
  3.4 0.6 gather_fusion
  4.1 0.1 copy.14
  4.1 0.7 maximum_bitcast_fusion.gain_ref
  4.8 108.6 %gather.13 = (bf16[8,4,2,4,2,2,3,16,384]{8,7,6,5,4,3,2,1,0:T(8,128)(2,1)}, f32[8,8,128]{2,1,0:T(8,128)}) custom-call(bf16[1,2,3,16,1536]{4,3,2,1,0:T(8,128)(2,1)} %bitcast.20, f32[1,8,128]{2,1,0:T(8,128)} %maximum_bitcast_fusion.gain_ref), custom_call_target="tpu_custom_call" | custom-call | tf_op jit(solution)/shard_map/gather/pallas_call | solution.py:230
  113.5 70.6 %phases.1 = (bf16[8,4,1536,384]{3,2,1,0:T(8,128)(2,1)}, f32[8,8,128]{2,1,0:T(8,128)}) custom-call(s32[1]{0:T(128)} %bitcast.place_ref, bf16[2,3,128,1536]{3,2,1,0:T(8,128)(2,1)} %clip_ref.1, s32[3,2,3,128]{3,2,1,0:T(4,128)} %copy.15.pos_ref, bf16[2,3,128,1536]{3,2,1,0:T(8,128)(2,1)} %cot_ref.1, f32[8,8,128]{2,1,0:T(8,128)} %get-tuple-element.8.gains_ref, ...), custom_call_target="tpu_custom_call" | custom-call | tf_op jit(solution)/shard_map/phases/pallas_call | solution.py:689
  184.1 123.1 %scatter.1 = (f32[2,3,16,1536]{3,2,1,0:T(8,128)}, f32[8,128]{1,0:T(8,128)}) custom-call(bf16[8,4,2,4,2,2,3,16,384]{8,7,6,5,4,3,2,1,0:T(8,128)(2,1)} %bitcast.17, f32[8,8,128]{2,1,0:T(8,128)} %get-tuple-element.11.dgain_ref), custom_call_target="tpu_custom_call" | custom-call | tf_op jit(solution)/shard_map/scatter/pallas_call | solution.py:506
  307.3 0.7 slice.7
  307.9 0.1 copy.16
  308.1 0.6 gather_fusion.1
  308.7 0.1 copy.17
  308.8 1.3 fusion
  310.0 1.9 copy.19
  (1 shorter events, 0.0 us)

commit v4 on v1

v4 whole, which is shorter than its diff:
```python
import functools
import math

import jax
import jax.numpy as jnp
import numpy as np
from jax import lax
from jax.experimental import pallas as pl
from jax.experimental.pallas import tpu as pltpu
from jax.sharding import PartitionSpec as P

D = 1536
HEAD = 128
TOK = 128
HEADS = D // HEAD
PHASES = 8
F32 = jnp.float32
BF16 = jnp.bfloat16

NN = (((1,), (0,)), ((), ()))
NT = (((1,), (1,)), ((), ()))
TN = (((0,), (0,)), ((), ()))


def dot(a, b, dims=NN, precision=None):
    return lax.dot_general(a, b, dims, precision=precision, preferred_element_type=F32)


def rotary_constants():
    first = HEAD // 8
    rest = (HEAD - first) // 2
    freq = np.zeros((8, HEAD), np.float32)
    partner = np.zeros(HEAD, np.int32)
    sign = np.zeros((1, HEAD), np.float32)
    offset = 0
    for axis, width in enumerate((first, rest, rest)):
        half = width // 2
        values = np.float32(256.0) ** (np.float32(-2.0) * np.arange(half, dtype=np.float32) / np.float32(width))
        low = np.arange(offset, offset + half)
        high = low + half
        freq[axis, low] = values
        freq[axis, high] = values
        partner[low], partner[high] = high, low
        sign[0, low], sign[0, high] = -1.0, 1.0
        offset += width
    swap = np.zeros((HEAD, HEAD), np.float32)
    swap[partner, np.arange(HEAD)] = 1.0
    return freq, swap, sign


MESH = pl.DeviceIdType.MESH
AXES = "xyz"
GATHER_LAG = 2
GATHER_BASE = (0, 9, 15, 21, 27, 33)
ORDERS = ("xyz", "yzx", "zxy")


class Place:
    def __init__(self):
        self.pipe = lax.axis_index("pipe")
        self.dp = lax.axis_index("dp")
        self.core = self.dp % 2
        self.at = {
            "x": self.dp // 8 * 2 + self.pipe % 2,
            "y": self.pipe // 2,
            "z": self.dp // 2 % 4,
        }

    def device(self, core=None, **moved):
        c = {**self.at, **moved}
        core = self.core if core is None else core
        return (c["y"] * 2 + c["x"] % 2, (c["x"] // 2 * 4 + c["z"]) * 2 + core)

    def step(self, axis, delta):
        return (self.at[axis] + delta + 4) % 4

    def neighbour(self, axis, delta):
        return self.device(**{axis: self.step(axis, delta)})

    def sibling(self):
        return self.device(core=1 - self.core)


def greet(place):
    barrier = pltpu.get_barrier_semaphore()
    others = [place.neighbour(axis, delta) for axis in AXES for delta in (1, -1, 2)]
    others.append(place.sibling())
    others += [((place.pipe + q) % PHASES, place.dp) for q in range(1, PHASES)]
    others += [(place.pipe, (place.dp + q) % WIDE_PEERS) for q in range(1, WIDE_PEERS)]
    for other in others:
        pl.semaphore_signal(barrier, inc=1, device_id=other, device_id_type=MESH)
    pl.semaphore_wait(barrier, len(others))


WHOLE = "whole"


def half(h):
    return ("half", h)


def block(ref, lead, k, core, x, y, z):
    def plain(v):
        if v is WHOLE:
            return slice(None)
        return pl.ds(2 * v[1], 2) if isinstance(v, tuple) else v

    if x is WHOLE:
        xh, xl = slice(None), slice(None)
    elif isinstance(x, tuple):
        xh, xl = x[1], slice(None)
    else:
        xh, xl = x // 2, x % 2
    return ref.at[(*lead, plain(y), xh, plain(z), core, xl, k)]


TILES = (4, 2, 4, 2, 2, 3, 16, D // 4)


class Gather:
    def __init__(self, place, shard, gain, weights, gains, sems):
        self.place, self.shard, self.gain, self.weights, self.gains = place, shard, gain, weights, gains
        (self.first_send, self.first_recv, self.gain_send, self.gain_recv, self.own_sem, self.send, self.recv) = sems

    def piece(self, q):
        return self.shard.at[0, q % 2, :, :, pl.ds(pl.multiple_of(q // 2 * (D // 4), 128), D // 4)]

    def spot(self, owner, q):
        place = self.place
        return self.weights.at[owner, q // 2, place.dp // 8, place.dp // 2 % 4, place.core, q % 2]

    def first(self, q, owner, target):
        return pltpu.make_async_remote_copy(
            src_ref=self.piece(q), dst_ref=self.spot(owner, q),
            send_sem=self.first_send.at[q], recv_sem=self.first_recv.at[owner],
            device_id=(target, self.place.dp), device_id_type=MESH)

    def gain_copy(self, owner, q):
        return pltpu.make_async_remote_copy(
            src_ref=self.gain.at[0], dst_ref=self.gains.at[owner],
            send_sem=self.gain_send.at[q], recv_sem=self.gain_recv.at[owner],
            device_id=(q, self.place.dp), device_id_type=MESH)

    def spread(self):
        me = self.place.pipe
        own = pltpu.make_async_copy(self.piece(me), self.spot(me, me), self.own_sem.at[0])
        own.start()
        for q in range(PHASES):
            @pl.when(q != me)
            def _():
                self.first(q, me, q).start()
                self.gain_copy(me, q).start()

            @pl.when(q == me)
            def _():
                self.gains[q] = self.gain[0]
        own.wait()

    def spread_wait(self):
        for q in range(PHASES):
            @pl.when(q != self.place.pipe)
            def _():
                self.first(q, self.place.pipe, q).wait_send()
                self.gain_copy(self.place.pipe, q).wait_send()
                self.first(q, q, q).wait_recv()
                self.gain_copy(q, q).wait_recv()

    def copies(self, stage, s, parity):
        place = self.place
        made = []

        def add(view, device):
            i = GATHER_BASE[stage] + len(made)
            made.append(pltpu.make_async_remote_copy(
                src_ref=view, dst_ref=view, send_sem=self.send.at[parity, i], recv_sem=self.recv.at[parity, i],
                device_id=device, device_id_type=MESH))

        if stage == 5:
            add(self.weights.at[s, :, :, :, place.core], place.sibling())
            return made
        for k, (a, b, c) in enumerate(ORDERS):
            def view(**where):
                return block(self.weights, (s,), k, place.core, **{**place.at, **where})

            if stage == 0:
                for delta in (1, -1, 2):
                    add(view(), place.neighbour(c, delta))
            elif stage == 1:
                for delta in (1, -1):
                    add(view(**{c: WHOLE}), place.neighbour(b, delta))
            elif stage == 2:
                for h, delta in enumerate((1, -1)):
                    add(view(**{b: place.step(b, -delta), c: half(h)}), place.neighbour(b, delta))
            elif stage == 3:
                for delta in (1, -1):
                    add(view(**{b: WHOLE, c: WHOLE}), place.neighbour(a, delta))
            else:
                for h, delta in enumerate((1, -1)):
                    add(view(**{a: place.step(a, -delta), b: half(h), c: WHOLE}), place.neighbour(a, delta))
        return made

    def tick(self, t):
        for stage in reversed(range(7)):
            s = t - GATHER_LAG * stage

            @pl.when((s >= 0) & (s < PHASES))
            def _():
                if stage:
                    for copy in self.copies(stage - 1, s, (t + GATHER_LAG) % (2 * GATHER_LAG)):
                        copy.wait()
                if stage < 6:
                    for copy in self.copies(stage, s, t % (2 * GATHER_LAG)):
                        copy.start()


STRIP = (3, 16, D // 4)
STAGE_BASE = (0, 1, 7, 13, 19, 25)
WIDE_PEERS = 16


def cut(ref, lead, k, where):
    index = []
    for axis in ORDERS[k]:
        if axis in where:
            v = where[axis]
            index.append(pl.ds(2 * v[1], 2) if isinstance(v, tuple) else v)
    return ref.at[(*lead, *index)]


def add_into(out, *parts):
    total = parts[0][...].astype(F32)
    for part in parts[1:]:
        total += part[...].astype(F32)
    out[...] = total.astype(out.dtype)


class Scatter:
    def __init__(self, place, bufs):
        self.place = place
        (self.grad, self.pair, self.wide, self.wide_half, self.wide_got, self.slim, self.slim_half,
         self.slim_got, self.last, self.last_got, self.final, self.out, self.send, self.recv,
         self.final_send, self.final_recv) = bufs

    def copies(self, stage, i):
        place, slot = self.place, i % 2
        made = []

        def add(src, dst, device):
            j = STAGE_BASE[stage] + len(made)
            made.append(pltpu.make_async_remote_copy(
                src_ref=src, dst_ref=dst, send_sem=self.send.at[slot, j], recv_sem=self.recv.at[slot, j],
                device_id=device, device_id_type=MESH))

        if stage == 0:
            add(self.grad.at[slot, :, :, :, 1 - place.core], self.pair.at[slot], place.sibling())
            return made
        for k, (a, b, c) in enumerate(ORDERS):
            if stage == 1:
                for h, delta in enumerate((1, -1)):
                    src = cut(self.wide, (slot, k), k, {a: place.step(a, 2), b: half(h)})
                    add(src, self.wide_half.at[slot, k, h], place.neighbour(a, delta))
            elif stage == 2:
                for h, delta in enumerate((1, -1)):
                    src = cut(self.wide, (slot, k), k, {a: place.step(a, delta)})
                    add(src, self.wide_got.at[slot, k, h], place.neighbour(a, delta))
            elif stage == 3:
                for h, delta in enumerate((1, -1)):
                    src = self.slim.at[slot, k, place.step(b, 2), pl.ds(2 * h, 2)]
                    add(src, self.slim_half.at[slot, k, h], place.neighbour(b, delta))
            elif stage == 4:
                for h, delta in enumerate((1, -1)):
                    src = self.slim.at[slot, k, place.step(b, delta)]
                    add(src, self.slim_got.at[slot, k, h], place.neighbour(b, delta))
            else:
                for h, delta in enumerate((1, -1, 2)):
                    src = self.last.at[slot, k, place.step(c, delta)]
                    add(src, self.last_got.at[slot, k, h], place.neighbour(c, delta))
        return made

    def fill_wide(self, i):
        slot = i % 2
        core = self.place.core

        def row(y, carry):
            for xh in range(2):
                for xl in range(2):
                    x = xh * 2 + xl
                    for k in range(3):
                        full = slice(None)
                        where = {"x": x, "y": y, "z": full}
                        out = self.wide.at[(slot, k, *(where[axis] for axis in ORDERS[k]))]
                        add_into(out, self.grad.at[slot, y, xh, :, core, xl, k], self.pair.at[slot, y, xh, :, xl, k])
            return carry

        lax.fori_loop(0, 4, row, 0)

    def process(self, stage, i):
        place, slot = self.place, i % 2
        if stage == 1:
            self.fill_wide(i)
            return
        for k, (a, b, c) in enumerate(ORDERS):
            if stage == 2:
                for h, delta in enumerate((1, -1)):
                    part = self.wide.at[slot, k, place.step(a, delta), pl.ds(2 * h, 2)]
                    add_into(part, part, self.wide_half.at[slot, k, h])
            elif stage == 3:
                add_into(self.slim.at[slot, k], self.wide.at[slot, k, place.at[a]],
                         self.wide_got.at[slot, k, 0], self.wide_got.at[slot, k, 1])
            elif stage == 4:
                for h, delta in enumerate((1, -1)):
                    part = self.slim.at[slot, k, place.step(b, delta), pl.ds(2 * h, 2)]
                    add_into(part, part, self.slim_half.at[slot, k, h])
            elif stage == 5:
                add_into(self.last.at[slot, k], self.slim.at[slot, k, place.at[b]],
                         self.slim_got.at[slot, k, 0], self.slim_got.at[slot, k, 1])
            else:
                add_into(self.final.at[PHASES - 1 - i, k], self.last.at[slot, k, place.at[c]],
                         *(self.last_got.at[slot, k, h] for h in range(3)))

    def final_copy(self, s, source, target):
        return pltpu.make_async_remote_copy(
            src_ref=self.final.at[s], dst_ref=self.out.at[source],
            send_sem=self.final_send.at[s], recv_sem=self.final_recv.at[source],
            device_id=(target, self.place.dp), device_id_type=MESH)

    def deliver(self, i):
        me, s = self.place.pipe, PHASES - 1 - i

        @pl.when(s != me)
        def _():
            self.final_copy(s, me, s).start()

        @pl.when(s == me)
        def _():
            self.out[s] = self.final[s]

    def settle(self):
        for q in range(PHASES):
            @pl.when(q != self.place.pipe)
            def _():
                self.final_copy(q, q, q).wait()

    def tick(self, t, first):
        for stage in reversed(range(7)):
            i = t - first - stage

            @pl.when((i >= 0) & (i < PHASES))
            def _():
                if stage:
                    for copy in self.copies(stage - 1, i):
                        copy.wait()
                    self.process(stage, i)
                if stage < 6:
                    for copy in self.copies(stage, i):
                        copy.start()
                else:
                    self.deliver(i)


class GainSum:
    def __init__(self, place, dgains, bufs):
        self.place, self.dgains = place, dgains
        (self.rows, self.wide, self.sum, self.send, self.recv, self.wide_send, self.wide_recv) = bufs

    def narrow(self, owner, source, target):
        return pltpu.make_async_remote_copy(
            src_ref=self.dgains.at[owner], dst_ref=self.rows.at[source],
            send_sem=self.send.at[owner], recv_sem=self.recv.at[source],
            device_id=(target, self.place.dp), device_id_type=MESH)

    def share(self, index, source, target):
        return pltpu.make_async_remote_copy(
            src_ref=self.sum, dst_ref=self.wide.at[source],
            send_sem=self.wide_send.at[index], recv_sem=self.wide_recv.at[source],
            device_id=(self.place.pipe, target), device_id_type=MESH)

    def start(self):
        me = self.place.pipe
        for q in range(PHASES):
            @pl.when(q != me)
            def _():
                self.narrow(q, me, q).start()

            @pl.when(q == me)
            def _():
                self.rows[q] = self.dgains[q]

    def middle(self):
        for q in range(PHASES):
            @pl.when(q != self.place.pipe)
            def _():
                self.narrow(q, q, q).wait()
        self.sum[...] = jnp.sum(self.rows[...], axis=0)
        for q in range(WIDE_PEERS):
            @pl.when(q != self.place.dp)
            def _():
                self.share(q, self.place.dp, q).start()

            @pl.when(q == self.place.dp)
            def _():
                self.wide[q] = self.sum[...]

    def finish(self, total):
        for q in range(WIDE_PEERS):
            @pl.when(q != self.place.dp)
            def _():
                self.share(q, q, q).wait()
        total[...] = jnp.sum(self.wide[...], axis=0)


def head(j):
    return pl.ds(j * HEAD, HEAD)


def forward_phase(s, w_ref, tabs, swap, hs, qs, ks, es, ms, ns, rcols, icols):
    a0, b0, a1, b1 = tabs
    ones = jnp.ones((TOK, HEAD), BF16)
    for j in range(HEADS):
        hj = hs[s, :, head(j)]
        hf = hj.astype(F32)
        r = lax.rsqrt(jnp.mean(hf * hf, axis=-1, keepdims=True) + 1e-6)
        rcols[s, :, j : j + 1] = r
        n = hf * r
        nsw = dot(hj, swap) * r
        ns[s, :, head(j)] = nsw.astype(BF16)
        qs[s, :, head(j)] = (n * a0 + nsw * b0).astype(BF16)
        ks[s, :, head(j)] = (n * a1 + nsw * b1).astype(BF16)
    for j in range(HEADS):
        scores = dot(qs[s, :, head(j)], ks[s, :, head(j)], NT)
        es[s, :, head(j)] = jnp.exp(scores).astype(BF16)
    for j in range(HEADS):
        both = dot(es[s, :, head(j)], jnp.concatenate([hs[s, :, head(j)], ones], axis=1))
        inv = 1.0 / both[:, HEAD:]
        icols[s, :, j : j + 1] = inv[:, 0:1]
        ms[s, :, head(j)] = (both[:, :HEAD] * inv).astype(BF16)
    for c in range(4):
        cols = pl.ds(c * 384, 384)
        update = dot(ms[s], w_ref[s % 2, c].reshape(D, D // 4))
        hs[s + 1, :, cols] = (hs[s, :, cols].astype(F32) + update).astype(BF16)


def backward_phase(s, w_ref, tabs, swap, g, gm, acc, hs, qs, ks, es, ms, ns, rcols, icols, grad_ref):
    a0, b0, a1, b1 = tabs
    for c in range(4):
        cols = pl.ds(c * 384, 384)
        total = None
        for y in range(4):
            part = dot(g[:, pl.ds(y * 384, 384)], w_ref[s % 2, y, c // 2, pl.ds(c % 2 * 2, 2)].reshape(384, D // 4), NT)
            total = part if total is None else total + part
        gm[:, cols] = total.astype(BF16)
    for y in range(4):
        cols = pl.ds(y * 384, 384)
        for t in range(4):
            rows = pl.ds(t * 384, 384)
            part = dot(ms[s, :, rows], g[:, cols], TN).astype(BF16)
            grad_ref[(s + 1) % 2, y, t // 2, pl.ds(t % 2 * 2, 2)] = part.reshape(2, 2, 2, *STRIP)
    acc[...] = jnp.zeros_like(acc)
    for j in range(HEADS):
        hj = hs[s, :, head(j)]
        ej = es[s, :, head(j)]
        qj = qs[s, :, head(j)]
        kj = ks[s, :, head(j)]
        r = rcols[s, :, j : j + 1]
        gmf = gm[:, head(j)].astype(F32) * icols[s, :, j : j + 1]
        delta = jnp.sum(gmf * ms[s, :, head(j)].astype(F32), axis=-1, keepdims=True)
        gmb = gmf.astype(BF16)
        ga = dot(gmb, hj, NT)
        ds = (ej.astype(F32) * (ga - delta)).astype(BF16)
        gv = dot(ej, gmb, TN)
        dq = dot(ds, kj)
        dk = dot(ds, qj, TN)
        n = hj.astype(F32) * r
        nsw = ns[s, :, head(j)].astype(F32)
        acc[0] += n * dq
        acc[1] += nsw * dq
        acc[2] += n * dk
        acc[3] += nsw * dk
        crossed = (dq * b0 + dk * b1).astype(BF16)
        dn = dq * a0 + dk * a1 + dot(crossed, swap, NT)
        dh = r * (dn - n * jnp.mean(dn * n, axis=-1, keepdims=True))
        g[:, head(j)] = (g[:, head(j)].astype(F32) + (dh + gv)).astype(BF16)


LIVE = 6


def window_kernel(shard_ref, gain_ref, clip_ref, pos_ref, cot_ref, freq_ref, swap_ref, sign_ref,
                  w_ref, out_ref, total_ref, *rest):
    rest = iter(rest)
    take = lambda count: [next(rest) for _ in range(count)]
    saved = take(8)
    g, gm, acc, cosine, sine, gains, dgains, wbuf = take(8)
    gather_sems = take(7)
    scatter_bufs = take(16)
    gain_bufs = take(7)
    in_sem, w_sem = take(2)
    grad = scatter_bufs[0]
    hs = saved[0]
    place = Place()
    live = place.pipe < LIVE
    slot = jnp.minimum(place.pipe, LIVE - 1)
    clip_in = pltpu.make_async_copy(clip_ref.at[slot // 3, slot % 3], hs.at[0], in_sem.at[0])
    cot_in = pltpu.make_async_copy(cot_ref.at[slot // 3, slot % 3], g, in_sem.at[1])
    clip_in.start()
    cot_in.start()
    greet(place)
    gather = Gather(place, shard_ref, gain_ref, w_ref, gains, gather_sems)
    scatter = Scatter(place, scatter_bufs)
    sums = GainSum(place, dgains, gain_bufs)
    scale = 1.0 / math.sqrt(HEAD)
    gather.spread()
    positions = pos_ref[:, slot // 3, slot % 3, :].astype(F32)
    padded = jnp.concatenate([positions, jnp.zeros((5, TOK), F32)], axis=0)
    angles = dot(padded, freq_ref[...], TN, lax.Precision.HIGHEST)
    cosine[...] = jnp.cos(angles)
    sine[...] = jnp.sin(angles) * sign_ref[...]

    @pl.when(jnp.logical_not(live))
    def _():
        grad[...] = jnp.zeros_like(grad)
        dgains[...] = jnp.zeros_like(dgains)

    clip_in.wait()
    cot_in.wait()
    gather.spread_wait()

    def tables(s):
        rows = gains[s]
        c, n = cosine[...], sine[...]
        return (c * (rows[0:1] * scale), n * (rows[2:3] * scale), c * rows[1:2], n * rows[3:4])

    def weights_in(s):
        return pltpu.make_async_copy(w_ref.at[s], wbuf.at[s % 2], w_sem.at[s % 2])

    arrive = 6 * GATHER_LAG

    def forward_tick(t, carry):
        gather.tick(t)
        s = t - arrive - 1

        @pl.when(s >= 0)
        def _():
            weights_in(s).wait()

            @pl.when(live)
            def _():
                forward_phase(s, wbuf, tables(s), swap_ref[...], *saved)

        ready = t - arrive

        @pl.when((ready >= 0) & (ready < PHASES))
        def _():
            weights_in(ready).start()

        return carry

    lax.fori_loop(0, PHASES + arrive + 1, forward_tick, 0)

    def backward_tick(t, carry):
        scatter.tick(t, 1)
        s = PHASES - 1 - t

        @pl.when((t >= 2) & (t < PHASES))
        def _():
            weights_in(s).wait()

        @pl.when(live & (t < PHASES))
        def _():
            backward_phase(s, wbuf, tables(s), swap_ref[...], g, gm, acc, *saved, grad)
            x0 = jnp.sum(acc[0] * cosine[...], axis=0, keepdims=True)
            y0 = jnp.sum(acc[1] * sine[...], axis=0, keepdims=True)
            x1 = jnp.sum(acc[2] * cosine[...], axis=0, keepdims=True)
            y1 = jnp.sum(acc[3] * sine[...], axis=0, keepdims=True)
            dgains[s] = jnp.concatenate([x0 * scale, x1, y0 * scale, y1, jnp.zeros((4, HEAD), F32)], axis=0)

        @pl.when(t < PHASES - 2)
        def _():
            weights_in(s - 2).start()

        @pl.when(t == PHASES)
        def _():
            sums.start()

        @pl.when(t == PHASES + 2)
        def _():
            sums.middle()

        return carry

    lax.fori_loop(0, PHASES + 7, backward_tick, 0)
    sums.finish(total_ref)
    scatter.settle()
    for y in range(4):
        for xl in range(2):
            out_ref[xl, :, :, pl.ds(y * (D // 4), D // 4)] = scatter.out[y * 2 + xl].astype(F32)


def window(shard, gain_rows, clips, positions, cotangent):
    freq, swap, sign = rotary_constants()
    piece = (16, D // 4)
    sems = pltpu.SemaphoreType.DMA
    vmem = pl.BlockSpec(memory_space=pltpu.VMEM)
    anywhere = pl.BlockSpec(memory_space=pl.ANY)
    rows = pltpu.VMEM((PHASES, TOK, D), BF16)
    columns = pltpu.VMEM((PHASES, TOK, HEAD), F32)
    scratch = [
        pltpu.VMEM((PHASES + 1, TOK, D), BF16), rows, rows, rows, rows, rows, columns, columns,
        pltpu.VMEM((TOK, D), BF16),
        pltpu.VMEM((TOK, D), BF16),
        pltpu.VMEM((4, TOK, HEAD), F32),
        pltpu.VMEM((TOK, HEAD), F32),
        pltpu.VMEM((TOK, HEAD), F32),
        pltpu.VMEM((PHASES, 8, HEAD), F32),
        pltpu.VMEM((PHASES, 8, HEAD), F32),
        pltpu.VMEM((2, *TILES), BF16),
        sems((PHASES,)), sems((PHASES,)), sems((PHASES,)), sems((PHASES,)), sems((1,)),
        sems((2 * GATHER_LAG, 34)), sems((2 * GATHER_LAG, 34)),
        pltpu.VMEM((2, *TILES), BF16),
        pltpu.VMEM((2, 4, 2, 4, 2, *STRIP), BF16),
        pltpu.VMEM((2, 3, 4, 4, 4, *piece), BF16),
        pltpu.VMEM((2, 3, 2, 2, 4, *piece), BF16),
        pltpu.VMEM((2, 3, 2, 4, 4, *piece), BF16),
        pltpu.VMEM((2, 3, 4, 4, *piece), BF16),
        pltpu.VMEM((2, 3, 2, 2, *piece), BF16),
        pltpu.VMEM((2, 3, 2, 4, *piece), BF16),
        pltpu.VMEM((2, 3, 4, *piece), BF16),
        pltpu.VMEM((2, 3, 3, *piece), BF16),
        pltpu.VMEM((PHASES, *STRIP), BF16),
        pltpu.VMEM((PHASES, *STRIP), BF16),
        sems((2, 34)), sems((2, 34)), sems((PHASES,)), sems((PHASES,)),
        pltpu.VMEM((PHASES, 8, HEAD), F32),
        pltpu.VMEM((WIDE_PEERS, 8, HEAD), F32),
        pltpu.VMEM((8, HEAD), F32),
        sems((PHASES,)), sems((PHASES,)), sems((WIDE_PEERS,)), sems((WIDE_PEERS,)),
        sems((2,)), sems((2,)),
    ]
    return pl.pallas_call(
        window_kernel,
        out_shape=(
            jax.ShapeDtypeStruct((PHASES, *TILES), BF16),
            jax.ShapeDtypeStruct((2, 3, 16, D), F32),
            jax.ShapeDtypeStruct((8, HEAD), F32),
        ),
        in_specs=[vmem, vmem, anywhere, vmem, anywhere, vmem, vmem, vmem],
        out_specs=[anywhere, vmem, vmem],
        scratch_shapes=scratch,
        compiler_params=pltpu.CompilerParams(
            collective_id=0, has_side_effects=True, vmem_limit_bytes=63 << 20
        ),
        name="window",
    )(
        shard, gain_rows, clips, positions, cotangent, jnp.asarray(freq),
        jnp.asarray(swap, BF16), jnp.asarray(sign),
    )


def shards(clips, positions, out_proj, qk_gains, cotangent):
    _, swap, _ = rotary_constants()
    partner = np.argmax(swap, axis=0)
    own = qk_gains[0].astype(F32)
    gain_rows = jnp.concatenate([own, own[:, partner], jnp.zeros((4, HEAD), F32)], axis=0)[None]
    _, shard, total = window(out_proj.reshape(1, 2, 3, 16, D), gain_rows, clips, positions, cotangent)
    dgain = total[0:2] + total[2:4][:, partner]
    return (shard.reshape(1, D // 16, D), dgain[None])


def solution(mesh):
    placed = (
        P(None, None, "dp", None),
        P(None, None, None, "dp"),
        P("pipe", "dp", None),
        P("pipe", None, None),
        P(None, None, "dp", None),
    )
    return jax.shard_map(
        shards,
        mesh=mesh,
        in_specs=placed,
        out_specs=(P("pipe", "dp", None), P("pipe", None, None)),
        check_vma=False,
    )
```

time: 1030 us -> 228 us (0.22)
  waiting for transfers between devices: 856 us -> 0 us
  Pallas kernels: 70.2 us -> 218 us
  blocking collectives: 85.6 us -> 0 us
  between operations: 14.1 us -> 0.65 us
    reduce_scatter x1 -> x0, waiting for transfers between devices: 635 us -> none  [shards(): lax.psum_scatter(grads.reshape(PHASES * D, D), ('pipe', 'dp'), scatter_di...]
    all_gather x1 -> x0, waiting for transfers between devices: 220 us -> none  [shards(): lax.all_gather(out_proj[0], ('pipe', 'dp'), axis=0, tiled=True)]
    pallas_call x1, Pallas kernels: 70.2 us -> 218 us  [window(): pl.pallas_call(window_kernel, out_shape=(jax.ShapeDtypeStruct((PHASES, *T...]
    psum x1 -> x0, blocking collectives: 66.2 us -> none  [shards(): total = lax.psum(dgains, ('pipe', 'dp'))]
    all_gather x1 -> x0, blocking collectives: 19.3 us -> none  [shards(): gains = lax.all_gather(qk_gains[0], 'pipe', axis=0)]
  transfers between devices with their start and end apart: 2 -> 0, of which waited for: 2 -> 0; matrix products, arithmetic and copies ran while one was open for 0% -> 0% of each run, Pallas kernels for 0% -> 0%
where the time goes in v4:
time: 228 us
  Pallas kernels  218 us (96%)
  local copies, waits for them, and re-layouts  5.6 us (2%)
  other arithmetic  3.26 us (1%)
    pallas_call x1, Pallas kernels, window(): pl.pallas_call(window_kernel, out_shape=(jax.ShapeDtypeStruct((PHASES, *T...  218 us

profile of v4, /device:TPU:0, one launch (start us, length us, event | category | flops | bytes accessed | tf_op | source)
XLA Modules:
  0.0 228.0 jit_solution(13901512829065713519)
XLA Ops:
  0.6 0.1 pad.2.clone
  0.7 0.7 bitcast_convert_fusion
  1.4 0.7 pad_clamp_fusion
  2.0 1.3 copy.15.pos_ref
  3.3 0.1 copy.13
  3.4 0.6 gather_fusion
  4.1 0.1 copy.14
  4.1 0.7 maximum_bitcast_fusion.gain_ref
  4.8 218.5 %window.1 = (bf16[8,4,2,4,2,2,3,16,384]{8,7,6,5,4,3,2,1,0:T(8,128)(2,1)}, f32[2,3,16,1536]{3,2,1,0:T(8,128)}, f32[8,128]{1,0:T(8,128)}) custom-call(bf16[1,2,3,16,1536]{4,3,2,1,0:T(8,128)(2,1)} %bitcast.15, f32[1,8,128]{2,1,0:T(8,128)} %maximum_bitcast_fusion.gain_ref, bf16[2,3,128,1536]{3,2,1,0:T(8,128)(2,1)} %clip_ref.1, s32[3,2,3,128]{3,2,1,0:T(4,128)} %copy.15.pos_ref, ...), custom_call_target="tpu_custom_call" | custom-call | tf_op jit(solution)/shard_map/window/pallas_call | solution.py:638
  223.3 0.7 slice.7
  224.0 0.1 copy.16
  224.1 0.6 gather_fusion.1
  224.8 0.1 copy.17
  224.8 1.3 fusion
  226.1 1.9 copy.19
  (1 shorter events, 0.0 us)

commit v5 on v4

--- a/solution.py
+++ b/solution.py
@@ -50,7 +50,9 @@
 
 MESH = pl.DeviceIdType.MESH
 AXES = "xyz"
-GATHER_LAG = 2
+GATHER_GROUP = 4
+GATHER_GROUPED = 3
+GATHER_START = (0, 2, 4, 6, 8, 10, 12)
 GATHER_BASE = (0, 9, 15, 21, 27, 33)
 ORDERS = ("xyz", "yzx", "zxy")
 
@@ -137,14 +139,17 @@
 
     def gain_copy(self, owner, q):
         return pltpu.make_async_remote_copy(
-            src_ref=self.gain.at[0], dst_ref=self.gains.at[owner],
+            src_ref=self.gain, dst_ref=self.gains.at[owner],
             send_sem=self.gain_send.at[q], recv_sem=self.gain_recv.at[owner],
             device_id=(q, self.place.dp), device_id_type=MESH)
 
+    def own_copy(self):
+        me = self.place.pipe
+        return pltpu.make_async_copy(self.piece(me), self.spot(me, me), self.own_sem.at[0])
+
     def spread(self):
         me = self.place.pipe
-        own = pltpu.make_async_copy(self.piece(me), self.spot(me, me), self.own_sem.at[0])
-        own.start()
+        self.own_copy().start()
         for q in range(PHASES):
             @pl.when(q != me)
             def _():
@@ -153,26 +158,33 @@
 
             @pl.when(q == me)
             def _():
-                self.gains[q] = self.gain[0]
-        own.wait()
-
-    def spread_wait(self):
+                self.gains[q] = self.gain[...]
+
+    def arrived(self, s):
+        @pl.when(s != self.place.pipe)
+        def _():
+            self.first(s, s, s).wait_recv()
+
+        @pl.when(s == self.place.pipe)
+        def _():
+            self.own_copy().wait()
+
+    def gains_arrived(self):
         for q in range(PHASES):
             @pl.when(q != self.place.pipe)
             def _():
                 self.first(q, self.place.pipe, q).wait_send()
                 self.gain_copy(self.place.pipe, q).wait_send()
-                self.first(q, q, q).wait_recv()
                 self.gain_copy(q, q).wait_recv()
 
-    def copies(self, stage, s, parity):
+    def copies(self, stage, s):
         place = self.place
         made = []
 
         def add(view, device):
             i = GATHER_BASE[stage] + len(made)
             made.append(pltpu.make_async_remote_copy(
-                src_ref=view, dst_ref=view, send_sem=self.send.at[parity, i], recv_sem=self.recv.at[parity, i],
+                src_ref=view, dst_ref=view, send_sem=self.send.at[s, i], recv_sem=self.recv.at[s, i],
                 device_id=device, device_id_type=MESH))
 
         if stage == 5:
@@ -200,17 +212,30 @@
         return made
 
     def tick(self, t):
+        def move(stage, s):
+            if stage:
+                for copy in self.copies(stage - 1, s):
+                    copy.wait()
+            else:
+                self.arrived(s)
+            if stage < 6:
+                for copy in self.copies(stage, s):
+                    copy.start()
+
         for stage in reversed(range(7)):
-            s = t - GATHER_LAG * stage
-
-            @pl.when((s >= 0) & (s < PHASES))
-            def _():
-                if stage:
-                    for copy in self.copies(stage - 1, s, (t + GATHER_LAG) % (2 * GATHER_LAG)):
-                        copy.wait()
-                if stage < 6:
-                    for copy in self.copies(stage, s, t % (2 * GATHER_LAG)):
-                        copy.start()
+            turn = t - GATHER_START[stage]
+            if stage < GATHER_GROUPED:
+                @pl.when((turn >= 0) & (turn < PHASES // GATHER_GROUP))
+                def _():
+                    def one(n, carry):
+                        move(stage, turn * GATHER_GROUP + n)
+                        return carry
+
+                    lax.fori_loop(0, GATHER_GROUP, one, 0)
+            else:
+                @pl.when((turn >= 0) & (turn < PHASES))
+                def _():
+                    move(stage, turn)
 
 
 STRIP = (3, 16, D // 4)
@@ -234,6 +259,10 @@
     out[...] = total.astype(out.dtype)
 
 
+SCATTER_START = (0, 1, 3, 5, 6, 7, 8)
+WIDE_SLOTS = 4
+
+
 class Scatter:
     def __init__(self, place, bufs):
         self.place = place
@@ -242,27 +271,27 @@
          self.final_send, self.final_recv) = bufs
 
     def copies(self, stage, i):
-        place, slot = self.place, i % 2
+        place, slot, broad, sem = self.place, i % 2, i % WIDE_SLOTS, i % 4
         made = []
 
         def add(src, dst, device):
             j = STAGE_BASE[stage] + len(made)
             made.append(pltpu.make_async_remote_copy(
-                src_ref=src, dst_ref=dst, send_sem=self.send.at[slot, j], recv_sem=self.recv.at[slot, j],
+                src_ref=src, dst_ref=dst, send_sem=self.send.at[sem, j], recv_sem=self.recv.at[sem, j],
                 device_id=device, device_id_type=MESH))
 
         if stage == 0:
-            add(self.grad.at[slot, :, :, :, 1 - place.core], self.pair.at[slot], place.sibling())
+            add(self.grad.at[:, :, :, 1 - place.core], self.pair.at[slot], place.sibling())
             return made
         for k, (a, b, c) in enumerate(ORDERS):
             if stage == 1:
                 for h, delta in enumerate((1, -1)):
-                    src = cut(self.wide, (slot, k), k, {a: place.step(a, 2), b: half(h)})
-                    add(src, self.wide_half.at[slot, k, h], place.neighbour(a, delta))
+                    src = cut(self.wide, (broad, k), k, {a: place.step(a, 2), b: half(h)})
+                    add(src, self.wide_half.at[broad, k, h], place.neighbour(a, delta))
             elif stage == 2:
                 for h, delta in enumerate((1, -1)):
-                    src = cut(self.wide, (slot, k), k, {a: place.step(a, delta)})
-                    add(src, self.wide_got.at[slot, k, h], place.neighbour(a, delta))
+                    src = cut(self.wide, (broad, k), k, {a: place.step(a, delta)})
+                    add(src, self.wide_got.at[broad, k, h], place.neighbour(a, delta))
             elif stage == 3:
                 for h, delta in enumerate((1, -1)):
                     src = self.slim.at[slot, k, place.step(b, 2), pl.ds(2 * h, 2)]
@@ -278,7 +307,7 @@
         return made
 
     def fill_wide(self, i):
-        slot = i % 2
+        slot, broad = i % 2, i % WIDE_SLOTS
         core = self.place.core
 
         def row(y, carry):
@@ -288,25 +317,25 @@
                     for k in range(3):
                         full = slice(None)
                         where = {"x": x, "y": y, "z": full}
-                        out = self.wide.at[(slot, k, *(where[axis] for axis in ORDERS[k]))]
-                        add_into(out, self.grad.at[slot, y, xh, :, core, xl, k], self.pair.at[slot, y, xh, :, xl, k])
+                        out = self.wide.at[(broad, k, *(where[axis] for axis in ORDERS[k]))]
+                        add_into(out, self.grad.at[y, xh, :, core, xl, k], self.pair.at[slot, y, xh, :, xl, k])
             return carry
 
         lax.fori_loop(0, 4, row, 0)
 
     def process(self, stage, i):
-        place, slot = self.place, i % 2
+        place, slot, broad = self.place, i % 2, i % WIDE_SLOTS
         if stage == 1:
             self.fill_wide(i)
             return
         for k, (a, b, c) in enumerate(ORDERS):
             if stage == 2:
                 for h, delta in enumerate((1, -1)):
-                    part = self.wide.at[slot, k, place.step(a, delta), pl.ds(2 * h, 2)]
-                    add_into(part, part, self.wide_half.at[slot, k, h])
+                    part = self.wide.at[broad, k, place.step(a, delta), pl.ds(2 * h, 2)]
+                    add_into(part, part, self.wide_half.at[broad, k, h])
             elif stage == 3:
-                add_into(self.slim.at[slot, k], self.wide.at[slot, k, place.at[a]],
-                         self.wide_got.at[slot, k, 0], self.wide_got.at[slot, k, 1])
+                add_into(self.slim.at[slot, k], self.wide.at[broad, k, place.at[a]],
+                         self.wide_got.at[broad, k, 0], self.wide_got.at[broad, k, 1])
             elif stage == 4:
                 for h, delta in enumerate((1, -1)):
                     part = self.slim.at[slot, k, place.step(b, delta), pl.ds(2 * h, 2)]
@@ -341,22 +370,25 @@
             def _():
                 self.final_copy(q, q, q).wait()
 
-    def tick(self, t, first):
-        for stage in reversed(range(7)):
-            i = t - first - stage
+    def tick(self, t):
+        for stage in range(6, 0, -1):
+            i = t - SCATTER_START[stage]
 
             @pl.when((i >= 0) & (i < PHASES))
             def _():
-                if stage:
-                    for copy in self.copies(stage - 1, i):
-                        copy.wait()
-                    self.process(stage, i)
+                for copy in self.copies(stage - 1, i):
+                    copy.wait()
+                self.process(stage, i)
                 if stage < 6:
                     for copy in self.copies(stage, i):
                         copy.start()
                 else:
                     self.deliver(i)
 
+    def begin(self, i):
+        for copy in self.copies(0, i):
+            copy.start()
+
 
 class GainSum:
     def __init__(self, place, dgains, bufs):
@@ -401,26 +433,28 @@
             def _():
                 self.wide[q] = self.sum[...]
 
-    def finish(self, total):
+    def finish(self, total, swap):
         for q in range(WIDE_PEERS):
             @pl.when(q != self.place.dp)
             def _():
                 self.share(q, q, q).wait()
-        total[...] = jnp.sum(self.wide[...], axis=0)
+        rows = jnp.sum(self.wide[...], axis=0)
+        moved = dot(rows, swap.astype(F32), NN, lax.Precision.HIGHEST)
+        total[0] = rows[0:2] + moved[2:4]
 
 
 def head(j):
     return pl.ds(j * HEAD, HEAD)
 
 
-def forward_phase(s, w_ref, tabs, swap, hs, qs, ks, es, ms, ns, rcols, icols):
+def mix_phase(s, tabs, swap, hs, qs, ks, es, ms, ns, cols):
     a0, b0, a1, b1 = tabs
     ones = jnp.ones((TOK, HEAD), BF16)
     for j in range(HEADS):
         hj = hs[s, :, head(j)]
         hf = hj.astype(F32)
         r = lax.rsqrt(jnp.mean(hf * hf, axis=-1, keepdims=True) + 1e-6)
-        rcols[s, :, j : j + 1] = r
+        cols[s, :, j : j + 1] = r
         n = hf * r
         nsw = dot(hj, swap) * r
         ns[s, :, head(j)] = nsw.astype(BF16)
@@ -432,37 +466,41 @@
     for j in range(HEADS):
         both = dot(es[s, :, head(j)], jnp.concatenate([hs[s, :, head(j)], ones], axis=1))
         inv = 1.0 / both[:, HEAD:]
-        icols[s, :, j : j + 1] = inv[:, 0:1]
+        cols[s, :, 16 + j : 17 + j] = inv[:, 0:1]
         ms[s, :, head(j)] = (both[:, :HEAD] * inv).astype(BF16)
+
+
+def project_phase(s, w_ref, hs, ms):
     for c in range(4):
         cols = pl.ds(c * 384, 384)
         update = dot(ms[s], w_ref[s % 2, c].reshape(D, D // 4))
         hs[s + 1, :, cols] = (hs[s, :, cols].astype(F32) + update).astype(BF16)
 
 
-def backward_phase(s, w_ref, tabs, swap, g, gm, acc, hs, qs, ks, es, ms, ns, rcols, icols, grad_ref):
+def weight_phase(s, g, ms, grad_ref):
+    for y in range(4):
+        for t in range(4):
+            part = dot(ms[s, :, pl.ds(t * 384, 384)], g[:, pl.ds(y * 384, 384)], TN).astype(BF16)
+            grad_ref[y, t // 2, pl.ds(t % 2 * 2, 2)] = part.reshape(2, 2, 2, *STRIP)
+
+
+def input_phase(s, w_ref, tabs, swap, g, gm, acc, hs, qs, ks, es, ms, ns, cols):
     a0, b0, a1, b1 = tabs
     for c in range(4):
-        cols = pl.ds(c * 384, 384)
         total = None
         for y in range(4):
-            part = dot(g[:, pl.ds(y * 384, 384)], w_ref[s % 2, y, c // 2, pl.ds(c % 2 * 2, 2)].reshape(384, D // 4), NT)
+            w = w_ref[s % 2, y, c // 2, pl.ds(c % 2 * 2, 2)].reshape(384, D // 4)
+            part = dot(g[:, pl.ds(y * 384, 384)], w, NT)
             total = part if total is None else total + part
-        gm[:, cols] = total.astype(BF16)
-    for y in range(4):
-        cols = pl.ds(y * 384, 384)
-        for t in range(4):
-            rows = pl.ds(t * 384, 384)
-            part = dot(ms[s, :, rows], g[:, cols], TN).astype(BF16)
-            grad_ref[(s + 1) % 2, y, t // 2, pl.ds(t % 2 * 2, 2)] = part.reshape(2, 2, 2, *STRIP)
+        gm[:, pl.ds(c * 384, 384)] = total.astype(BF16)
     acc[...] = jnp.zeros_like(acc)
     for j in range(HEADS):
         hj = hs[s, :, head(j)]
         ej = es[s, :, head(j)]
         qj = qs[s, :, head(j)]
         kj = ks[s, :, head(j)]
-        r = rcols[s, :, j : j + 1]
-        gmf = gm[:, head(j)].astype(F32) * icols[s, :, j : j + 1]
+        r = cols[s, :, j : j + 1]
+        gmf = gm[:, head(j)].astype(F32) * cols[s, :, 16 + j : 17 + j]
         delta = jnp.sum(gmf * ms[s, :, head(j)].astype(F32), axis=-1, keepdims=True)
         gmb = gmf.astype(BF16)
         ga = dot(gmb, hj, NT)
@@ -489,8 +527,8 @@
                   w_ref, out_ref, total_ref, *rest):
     rest = iter(rest)
     take = lambda count: [next(rest) for _ in range(count)]
-    saved = take(8)
-    g, gm, acc, cosine, sine, gains, dgains, wbuf = take(8)
+    saved = take(7)
+    g, gm, acc, cosine, sine, own_gains, gains, dgains, wbuf = take(9)
     gather_sems = take(7)
     scatter_bufs = take(16)
     gain_bufs = take(7)
@@ -504,13 +542,14 @@
     cot_in = pltpu.make_async_copy(cot_ref.at[slot // 3, slot % 3], g, in_sem.at[1])
     clip_in.start()
     cot_in.start()
+    own_gains[...] = jnp.concatenate([gain_ref[0].astype(F32), jnp.zeros((6, HEAD), F32)], axis=0)
     greet(place)
-    gather = Gather(place, shard_ref, gain_ref, w_ref, gains, gather_sems)
+    gather = Gather(place, shard_ref, own_gains, w_ref, gains, gather_sems)
     scatter = Scatter(place, scatter_bufs)
     sums = GainSum(place, dgains, gain_bufs)
     scale = 1.0 / math.sqrt(HEAD)
     gather.spread()
-    positions = pos_ref[:, slot // 3, slot % 3, :].astype(F32)
+    positions = pos_ref[:, slot % 3, slot // 3, :].astype(F32)
     padded = jnp.concatenate([positions, jnp.zeros((5, TOK), F32)], axis=0)
     angles = dot(padded, freq_ref[...], TN, lax.Precision.HIGHEST)
     cosine[...] = jnp.cos(angles)
@@ -523,60 +562,77 @@
 
     clip_in.wait()
     cot_in.wait()
-    gather.spread_wait()
 
     def tables(s):
         rows = gains[s]
+        moved = dot(rows.astype(BF16), swap_ref[...])
         c, n = cosine[...], sine[...]
-        return (c * (rows[0:1] * scale), n * (rows[2:3] * scale), c * rows[1:2], n * rows[3:4])
+        return (c * (rows[0:1] * scale), n * (moved[0:1] * scale), c * rows[1:2], n * moved[1:2])
 
     def weights_in(s):
         return pltpu.make_async_copy(w_ref.at[s], wbuf.at[s % 2], w_sem.at[s % 2])
 
-    arrive = 6 * GATHER_LAG
+    arrive = GATHER_START[6]
 
     def forward_tick(t, carry):
         gather.tick(t)
-        s = t - arrive - 1
-
-        @pl.when(s >= 0)
-        def _():
+        ready = t - arrive
+
+        @pl.when(ready >= 0)
+        def _():
+            weights_in(ready).start()
+
+        @pl.when(t == arrive - 3)
+        def _():
+            gather.gains_arrived()
+
+            @pl.when(live)
+            def _():
+                mix_phase(0, tables(0), swap_ref[...], *saved)
+
+        @pl.when(ready >= 1)
+        def _():
+            s = ready - 1
             weights_in(s).wait()
 
             @pl.when(live)
             def _():
-                forward_phase(s, wbuf, tables(s), swap_ref[...], *saved)
-
-        ready = t - arrive
-
-        @pl.when((ready >= 0) & (ready < PHASES))
-        def _():
-            weights_in(ready).start()
+                project_phase(s, wbuf, hs, saved[4])
+                mix_phase(s + 1, tables(s + 1), swap_ref[...], *saved)
 
         return carry
 
-    lax.fori_loop(0, PHASES + arrive + 1, forward_tick, 0)
+    lax.fori_loop(0, PHASES + arrive, forward_tick, 0)
 
     def backward_tick(t, carry):
-        scatter.tick(t, 1)
-        s = PHASES - 1 - t
-
-        @pl.when((t >= 2) & (t < PHASES))
-        def _():
-            weights_in(s).wait()
-
-        @pl.when(live & (t < PHASES))
-        def _():
-            backward_phase(s, wbuf, tables(s), swap_ref[...], g, gm, acc, *saved, grad)
-            x0 = jnp.sum(acc[0] * cosine[...], axis=0, keepdims=True)
-            y0 = jnp.sum(acc[1] * sine[...], axis=0, keepdims=True)
-            x1 = jnp.sum(acc[2] * cosine[...], axis=0, keepdims=True)
-            y1 = jnp.sum(acc[3] * sine[...], axis=0, keepdims=True)
-            dgains[s] = jnp.concatenate([x0 * scale, x1, y0 * scale, y1, jnp.zeros((4, HEAD), F32)], axis=0)
-
-        @pl.when(t < PHASES - 2)
-        def _():
-            weights_in(s - 2).start()
+        scatter.tick(t)
+
+        @pl.when(t < PHASES)
+        def _():
+            s = PHASES - 1 - t
+
+            @pl.when(live)
+            def _():
+                weight_phase(s, g, saved[4], grad)
+
+            scatter.begin(t)
+
+            @pl.when(t != 1)
+            def _():
+                weights_in(s).wait()
+
+            @pl.when(live)
+            def _():
+                input_phase(s, wbuf, tables(s), swap_ref[...], g, gm, acc, *saved)
+                x0 = jnp.sum(acc[0] * cosine[...], axis=0, keepdims=True)
+                y0 = jnp.sum(acc[1] * sine[...], axis=0, keepdims=True)
+                x1 = jnp.sum(acc[2] * cosine[...], axis=0, keepdims=True)
+                y1 = jnp.sum(acc[3] * sine[...], axis=0, keepdims=True)
+                dgains[s] = jnp.concatenate([x0 * scale, x1, y0 * scale, y1, jnp.zeros((4, HEAD), F32)], axis=0)
+
+            @pl.when(t < PHASES - 2)
+            def _():
+                weights_in(s - 2).start()
 
         @pl.when(t == PHASES)
         def _():
@@ -588,15 +644,15 @@
 
         return carry
 
-    lax.fori_loop(0, PHASES + 7, backward_tick, 0)
-    sums.finish(total_ref)
+    lax.fori_loop(0, PHASES + SCATTER_START[6], backward_tick, 0)
+    sums.finish(total_ref, swap_ref[...])
     scatter.settle()
     for y in range(4):
         for xl in range(2):
             out_ref[xl, :, :, pl.ds(y * (D // 4), D // 4)] = scatter.out[y * 2 + xl].astype(F32)
 
 
-def window(shard, gain_rows, clips, positions, cotangent):
+def window(shard, gain_pair, clips, positions, cotangent):
     freq, swap, sign = rotary_constants()
     piece = (16, D // 4)
     sems = pltpu.SemaphoreType.DMA
@@ -605,22 +661,23 @@
     rows = pltpu.VMEM((PHASES, TOK, D), BF16)
     columns = pltpu.VMEM((PHASES, TOK, HEAD), F32)
     scratch = [
-        pltpu.VMEM((PHASES + 1, TOK, D), BF16), rows, rows, rows, rows, rows, columns, columns,
+        rows, rows, rows, rows, rows, rows, columns,
         pltpu.VMEM((TOK, D), BF16),
         pltpu.VMEM((TOK, D), BF16),
         pltpu.VMEM((4, TOK, HEAD), F32),
         pltpu.VMEM((TOK, HEAD), F32),
         pltpu.VMEM((TOK, HEAD), F32),
+        pltpu.VMEM((8, HEAD), F32),
         pltpu.VMEM((PHASES, 8, HEAD), F32),
         pltpu.VMEM((PHASES, 8, HEAD), F32),
         pltpu.VMEM((2, *TILES), BF16),
         sems((PHASES,)), sems((PHASES,)), sems((PHASES,)), sems((PHASES,)), sems((1,)),
-        sems((2 * GATHER_LAG, 34)), sems((2 * GATHER_LAG, 34)),
-        pltpu.VMEM((2, *TILES), BF16),
+        sems((PHASES, 34)), sems((PHASES, 34)),
+        pltpu.VMEM(TILES, BF16),
         pltpu.VMEM((2, 4, 2, 4, 2, *STRIP), BF16),
-        pltpu.VMEM((2, 3, 4, 4, 4, *piece), BF16),
-        pltpu.VMEM((2, 3, 2, 2, 4, *piece), BF16),
-        pltpu.VMEM((2, 3, 2, 4, 4, *piece), BF16),
+        pltpu.VMEM((WIDE_SLOTS, 3, 4, 4, 4, *piece), BF16),
+        pltpu.VMEM((WIDE_SLOTS, 3, 2, 2, 4, *piece), BF16),
+        pltpu.VMEM((WIDE_SLOTS, 3, 2, 4, 4, *piece), BF16),
         pltpu.VMEM((2, 3, 4, 4, *piece), BF16),
         pltpu.VMEM((2, 3, 2, 2, *piece), BF16),
         pltpu.VMEM((2, 3, 2, 4, *piece), BF16),
@@ -628,7 +685,7 @@
         pltpu.VMEM((2, 3, 3, *piece), BF16),
         pltpu.VMEM((PHASES, *STRIP), BF16),
         pltpu.VMEM((PHASES, *STRIP), BF16),
-        sems((2, 34)), sems((2, 34)), sems((PHASES,)), sems((PHASES,)),
+        sems((4, 34)), sems((4, 34)), sems((PHASES,)), sems((PHASES,)),
         pltpu.VMEM((PHASES, 8, HEAD), F32),
         pltpu.VMEM((WIDE_PEERS, 8, HEAD), F32),
         pltpu.VMEM((8, HEAD), F32),
@@ -640,7 +697,7 @@
         out_shape=(
             jax.ShapeDtypeStruct((PHASES, *TILES), BF16),
             jax.ShapeDtypeStruct((2, 3, 16, D), F32),
-            jax.ShapeDtypeStruct((8, HEAD), F32),
+            jax.ShapeDtypeStruct((1, 2, HEAD), F32),
         ),
         in_specs=[vmem, vmem, anywhere, vmem, anywhere, vmem, vmem, vmem],
         out_specs=[anywhere, vmem, vmem],
@@ -650,19 +707,14 @@
         ),
         name="window",
     )(
-        shard, gain_rows, clips, positions, cotangent, jnp.asarray(freq),
+        shard, gain_pair, clips, positions.transpose(0, 2, 1, 3), cotangent, jnp.asarray(freq),
         jnp.asarray(swap, BF16), jnp.asarray(sign),
     )
 
 
 def shards(clips, positions, out_proj, qk_gains, cotangent):
-    _, swap, _ = rotary_constants()
-    partner = np.argmax(swap, axis=0)
-    own = qk_gains[0].astype(F32)
-    gain_rows = jnp.concatenate([own, own[:, partner], jnp.zeros((4, HEAD), F32)], axis=0)[None]
-    _, shard, total = window(out_proj.reshape(1, 2, 3, 16, D), gain_rows, clips, positions, cotangent)
-    dgain = total[0:2] + total[2:4][:, partner]
-    return (shard.reshape(1, D // 16, D), dgain[None])
+    _, shard, dgain = window(out_proj.reshape(1, 2, 3, 16, D), qk_gains, clips, positions, cotangent)
+    return (shard.reshape(1, D // 16, D), dgain)
 
 
 def solution(mesh):

time: 228 us -> 211 us (0.925)
  Pallas kernels: 218 us -> 207 us
  other arithmetic: 3.26 us -> 0 us
  local copies, waits for them, and re-layouts: 5.6 us -> 3.1 us
    pallas_call x1, Pallas kernels: 218 us -> 207 us  [window(): pl.pallas_call(window_kernel, out_shape=(jax.ShapeDtypeStruct((PHASES, *T...]
where the time goes in v5:
time: 211 us; the launch traced here: 210 us
  Pallas kernels  207 us (98%)
  local copies, waits for them, and re-layouts  3.1 us (1%)
    pallas_call x1, Pallas kernels, window(): pl.pallas_call(window_kernel, out_shape=(jax.ShapeDtypeStruct((PHASES, *T...  207 us

profile of v5, /device:TPU:0, one launch (start us, length us, event | category | flops | bytes accessed | tf_op | source)
XLA Modules:
  0.0 210.4 jit_solution(5634274562210398139)
XLA Ops:
  0.6 206.7 %window.1 = (bf16[8,4,2,4,2,2,3,16,384]{8,7,6,5,4,3,2,1,0:T(8,128)(2,1)}, f32[2,3,16,1536]{3,2,1,0:T(8,128)}, f32[1,2,128]{2,1,0:T(2,128)}) custom-call(bf16[1,2,3,16,1536]{4,3,2,1,0:T(8,128)(2,1)} %bitcast.4, bf16[1,2,128]{2,1,0:T(2,128)(2,1)} %gain_ref.1, bf16[2,3,128,1536]{3,2,1,0:T(8,128)(2,1)} %clip_ref.1, s32[3,3,2,128]{3,2,1,0:T(2,128)} %bitcast.5, ...), custom_call_target="tpu_custom_call" | custom-call | tf_op jit(solution)/shard_map/window/pallas_call | solution.py:695
  207.3 1.9 copy.12
  209.2 1.2 copy.13

commit v6 on v5

--- a/solution.py
+++ b/solution.py
@@ -253,6 +253,9 @@
 
 
 def add_into(out, *parts):
+    if len(parts) == 2:
+        out[...] = parts[0][...] + parts[1][...]
+        return
     total = parts[0][...].astype(F32)
     for part in parts[1:]:
         total += part[...].astype(F32)
@@ -484,7 +487,7 @@
             grad_ref[y, t // 2, pl.ds(t % 2 * 2, 2)] = part.reshape(2, 2, 2, *STRIP)
 
 
-def input_phase(s, w_ref, tabs, swap, g, gm, acc, hs, qs, ks, es, ms, ns, cols):
+def input_phase(s, w_ref, tabs, swap, g, gm, dsc, cosine, sine, hs, qs, ks, es, ms, ns, cols):
     a0, b0, a1, b1 = tabs
     for c in range(4):
         total = None
@@ -493,31 +496,35 @@
             part = dot(g[:, pl.ds(y * 384, 384)], w, NT)
             total = part if total is None else total + part
         gm[:, pl.ds(c * 384, 384)] = total.astype(BF16)
-    acc[...] = jnp.zeros_like(acc)
+    for j in range(HEADS):
+        gmf = gm[:, head(j)].astype(F32) * cols[s, :, 16 + j : 17 + j]
+        gmb = gmf.astype(BF16)
+        delta = jnp.sum(gmf * ms[s, :, head(j)].astype(F32), axis=-1, keepdims=True)
+        ga = dot(gmb, hs[s, :, head(j)], NT)
+        dsc[:, head(j)] = (es[s, :, head(j)].astype(F32) * (ga - delta)).astype(BF16)
+        gm[:, head(j)] = gmb
+    sums = [jnp.zeros((8, HEAD), F32)] * 4
+
+    def folded(total, value):
+        return total + jnp.sum(value.reshape(TOK // 8, 8, HEAD), axis=0)
+
     for j in range(HEADS):
         hj = hs[s, :, head(j)]
-        ej = es[s, :, head(j)]
-        qj = qs[s, :, head(j)]
-        kj = ks[s, :, head(j)]
         r = cols[s, :, j : j + 1]
-        gmf = gm[:, head(j)].astype(F32) * cols[s, :, 16 + j : 17 + j]
-        delta = jnp.sum(gmf * ms[s, :, head(j)].astype(F32), axis=-1, keepdims=True)
-        gmb = gmf.astype(BF16)
-        ga = dot(gmb, hj, NT)
-        ds = (ej.astype(F32) * (ga - delta)).astype(BF16)
-        gv = dot(ej, gmb, TN)
-        dq = dot(ds, kj)
-        dk = dot(ds, qj, TN)
+        ds = dsc[:, head(j)]
+        dq = dot(ds, ks[s, :, head(j)])
+        dk = dot(ds, qs[s, :, head(j)], TN)
         n = hj.astype(F32) * r
         nsw = ns[s, :, head(j)].astype(F32)
-        acc[0] += n * dq
-        acc[1] += nsw * dq
-        acc[2] += n * dk
-        acc[3] += nsw * dk
+        c, sn = cosine[...], sine[...]
+        nc, sc = n * c, nsw * sn
+        sums = [folded(t, v) for t, v in zip(sums, (nc * dq, sc * dq, nc * dk, sc * dk))]
         crossed = (dq * b0 + dk * b1).astype(BF16)
         dn = dq * a0 + dk * a1 + dot(crossed, swap, NT)
         dh = r * (dn - n * jnp.mean(dn * n, axis=-1, keepdims=True))
+        gv = dot(es[s, :, head(j)], gm[:, head(j)], TN)
         g[:, head(j)] = (g[:, head(j)].astype(F32) + (dh + gv)).astype(BF16)
+    return [jnp.sum(t, axis=0, keepdims=True) for t in sums]
 
 
 LIVE = 6
@@ -528,7 +535,7 @@
     rest = iter(rest)
     take = lambda count: [next(rest) for _ in range(count)]
     saved = take(7)
-    g, gm, acc, cosine, sine, own_gains, gains, dgains, wbuf = take(9)
+    g, gm, dsc, cosine, sine, own_gains, gains, dgains, wbuf = take(9)
     gather_sems = take(7)
     scatter_bufs = take(16)
     gain_bufs = take(7)
@@ -623,11 +630,7 @@
 
             @pl.when(live)
             def _():
-                input_phase(s, wbuf, tables(s), swap_ref[...], g, gm, acc, *saved)
-                x0 = jnp.sum(acc[0] * cosine[...], axis=0, keepdims=True)
-                y0 = jnp.sum(acc[1] * sine[...], axis=0, keepdims=True)
-                x1 = jnp.sum(acc[2] * cosine[...], axis=0, keepdims=True)
-                y1 = jnp.sum(acc[3] * sine[...], axis=0, keepdims=True)
+                x0, y0, x1, y1 = input_phase(s, wbuf, tables(s), swap_ref[...], g, gm, dsc, cosine, sine, *saved)
                 dgains[s] = jnp.concatenate([x0 * scale, x1, y0 * scale, y1, jnp.zeros((4, HEAD), F32)], axis=0)
 
             @pl.when(t < PHASES - 2)
@@ -664,7 +667,7 @@
         rows, rows, rows, rows, rows, rows, columns,
         pltpu.VMEM((TOK, D), BF16),
         pltpu.VMEM((TOK, D), BF16),
-        pltpu.VMEM((4, TOK, HEAD), F32),
+        pltpu.VMEM((TOK, D), BF16),
         pltpu.VMEM((TOK, HEAD), F32),
         pltpu.VMEM((TOK, HEAD), F32),
         pltpu.VMEM((8, HEAD), F32),

time: 211 us -> 206 us (0.976)
  Pallas kernels: 207 us -> 202 us
    pallas_call x1, Pallas kernels: 207 us -> 202 us  [window(): pl.pallas_call(window_kernel, out_shape=(jax.ShapeDtypeStruct((PHASES, *T...]
where the time goes in v6:
time: 206 us
  Pallas kernels  202 us (98%)
  local copies, waits for them, and re-layouts  3.1 us (2%)
    pallas_call x1, Pallas kernels, window(): pl.pallas_call(window_kernel, out_shape=(jax.ShapeDtypeStruct((PHASES, *T...  202 us

profile of v6, /device:TPU:0, one launch (start us, length us, event | category | flops | bytes accessed | tf_op | source)
XLA Modules:
  0.0 205.7 jit_solution(4794364704731684733)
XLA Ops:
  0.6 202.0 %window.1 = (bf16[8,4,2,4,2,2,3,16,384]{8,7,6,5,4,3,2,1,0:T(8,128)(2,1)}, f32[2,3,16,1536]{3,2,1,0:T(8,128)}, f32[1,2,128]{2,1,0:T(2,128)}) custom-call(bf16[1,2,3,16,1536]{4,3,2,1,0:T(8,128)(2,1)} %bitcast.4, bf16[1,2,128]{2,1,0:T(2,128)(2,1)} %gain_ref.1, bf16[2,3,128,1536]{3,2,1,0:T(8,128)(2,1)} %clip_ref.1, s32[3,3,2,128]{3,2,1,0:T(2,128)} %bitcast.5, ...), custom_call_target="tpu_custom_call" | custom-call | tf_op jit(solution)/shard_map/window/pallas_call | solution.py:698
  202.6 1.9 copy.12
  204.5 1.2 copy.13

commit v7 on v6

--- a/solution.py
+++ b/solution.py
@@ -450,7 +450,7 @@
     return pl.ds(j * HEAD, HEAD)
 
 
-def mix_phase(s, tabs, swap, hs, qs, ks, es, ms, ns, cols):
+def mix_phase(s, tabs, swap, hs, qs, ks, es, ms, ns, cols, mt):
     a0, b0, a1, b1 = tabs
     ones = jnp.ones((TOK, HEAD), BF16)
     for j in range(HEADS):
@@ -470,7 +470,9 @@
         both = dot(es[s, :, head(j)], jnp.concatenate([hs[s, :, head(j)], ones], axis=1))
         inv = 1.0 / both[:, HEAD:]
         cols[s, :, 16 + j : 17 + j] = inv[:, 0:1]
-        ms[s, :, head(j)] = (both[:, :HEAD] * inv).astype(BF16)
+        mixed = (both[:, :HEAD] * inv).astype(BF16)
+        ms[s, :, head(j)] = mixed
+        mt[s, head(j), :] = mixed.T
 
 
 def project_phase(s, w_ref, hs, ms):
@@ -480,14 +482,14 @@
         hs[s + 1, :, cols] = (hs[s, :, cols].astype(F32) + update).astype(BF16)
 
 
-def weight_phase(s, g, ms, grad_ref):
+def weight_phase(s, g, mt, grad_ref):
     for y in range(4):
         for t in range(4):
-            part = dot(ms[s, :, pl.ds(t * 384, 384)], g[:, pl.ds(y * 384, 384)], TN).astype(BF16)
+            part = dot(mt[s, pl.ds(t * 384, 384), :], g[:, pl.ds(y * 384, 384)]).astype(BF16)
             grad_ref[y, t // 2, pl.ds(t % 2 * 2, 2)] = part.reshape(2, 2, 2, *STRIP)
 
 
-def input_phase(s, w_ref, tabs, swap, g, gm, dsc, cosine, sine, hs, qs, ks, es, ms, ns, cols):
+def input_phase(s, w_ref, tabs, swap, g, gm, dsc, cosine, sine, hs, qs, ks, es, ms, ns, cols, mt):
     a0, b0, a1, b1 = tabs
     for c in range(4):
         total = None
@@ -534,7 +536,7 @@
                   w_ref, out_ref, total_ref, *rest):
     rest = iter(rest)
     take = lambda count: [next(rest) for _ in range(count)]
-    saved = take(7)
+    saved = take(8)
     g, gm, dsc, cosine, sine, own_gains, gains, dgains, wbuf = take(9)
     gather_sems = take(7)
     scatter_bufs = take(16)
@@ -620,7 +622,7 @@
 
             @pl.when(live)
             def _():
-                weight_phase(s, g, saved[4], grad)
+                weight_phase(s, g, saved[7], grad)
 
             scatter.begin(t)
 
@@ -664,7 +666,7 @@
     rows = pltpu.VMEM((PHASES, TOK, D), BF16)
     columns = pltpu.VMEM((PHASES, TOK, HEAD), F32)
     scratch = [
-        rows, rows, rows, rows, rows, rows, columns,
+        rows, rows, rows, rows, rows, rows, columns, pltpu.VMEM((PHASES, D, TOK), BF16),
         pltpu.VMEM((TOK, D), BF16),
         pltpu.VMEM((TOK, D), BF16),
         pltpu.VMEM((TOK, D), BF16),
@@ -706,7 +708,7 @@
         out_specs=[anywhere, vmem, vmem],
         scratch_shapes=scratch,
         compiler_params=pltpu.CompilerParams(
-            collective_id=0, has_side_effects=True, vmem_limit_bytes=63 << 20
+            collective_id=0, has_side_effects=True, vmem_limit_bytes=67_043_328
         ),
         name="window",
     )(

time: 206 us -> 206 us (level)
  no operation moved by 1% of the time
where the time goes in v7:
time: 206 us
  Pallas kernels  202 us (98%)
  local copies, waits for them, and re-layouts  3.1 us (2%)
    pallas_call x1, Pallas kernels, window(): pl.pallas_call(window_kernel, out_shape=(jax.ShapeDtypeStruct((PHASES, *T...  202 us

profile of v7, /device:TPU:0, one launch (start us, length us, event | category | flops | bytes accessed | tf_op | source)
XLA Modules:
  0.0 206.0 jit_solution(3110174167614332137)
XLA Ops:
  0.6 202.2 %window.1 = (bf16[8,4,2,4,2,2,3,16,384]{8,7,6,5,4,3,2,1,0:T(8,128)(2,1)}, f32[2,3,16,1536]{3,2,1,0:T(8,128)}, f32[1,2,128]{2,1,0:T(2,128)}) custom-call(bf16[1,2,3,16,1536]{4,3,2,1,0:T(8,128)(2,1)} %bitcast.4, bf16[1,2,128]{2,1,0:T(2,128)(2,1)} %gain_ref.1, bf16[2,3,128,1536]{3,2,1,0:T(8,128)(2,1)} %clip_ref.1, s32[3,3,2,128]{3,2,1,0:T(2,128)} %bitcast.5, ...), custom_call_target="tpu_custom_call" | custom-call | tf_op jit(solution)/shard_map/window/pallas_call | solution.py:700
  202.9 1.9 copy.12
  204.8 1.2 copy.13
